TPU v7x, 32 devices: a whole 2x2x4 slice. The times are simulated.
32 devices in a mesh: tm: 2 (over core), space: 16 (over z, y, x).
Axes of the slice: x: 2, y: 2, z: 4, core: 2. Of those that a mesh axis runs over, the one named last changes fastest.
Arguments:
- forcing: float32 [2, 4, 4, 8, 64, 640], P('tm', None, None, None, 'space'), may hold values from -6 to 6
- trajectory: float32 [2, 2, 8, 64, 640], P('tm', None, None, 'space'), may hold values from -0.45 to 0.45
- land_mask: int32 [8, 64, 640], P(None, 'space'), may hold values 0 or 1
- coupling: float32 [4, 4], replicated, may hold values from -0.6 to 0.6
Outputs:
- increments: float32 [2, 4, 4, 8, 64, 640], P('tm', None, None, None, 'space')
All inputs are finite; a program needn't handle non-finite values. No bound on the sum of `land_mask` on one device may be relied on, other than what follows from the above.
Results may differ from a plain program's by a relative error of at most 0.0001.
Values sent between devices are 32-bit elements; how exact they have to be, the bound alone decides.
No kernel may reach another device: no remote copies, remote signals or barrier semaphores. Data moves between devices by JAX's collectives and lax.ppermute only.
A program may use at most 64 MiB of HBM per device.

v0:
```python
import jax
import jax.numpy as jnp
from jax import lax
from jax.sharding import PartitionSpec as P

STEPS = 2


def extended(x, sides, width):
    for axis, dim in sides:
        count, length = (lax.axis_size(axis), x.shape[dim])
        up = [(i, (i + 1) % count) for i in range(count)]
        down = [(j, i) for i, j in up]
        last = lax.slice_in_dim(x, length - width, length, axis=dim)
        leading = lax.slice_in_dim(x, 0, width, axis=dim)
        before = lax.ppermute(last, axis, up)
        after = lax.ppermute(leading, axis, down)
        x = jnp.concatenate([before, x, after], axis=dim)
    return x


def from_behind(block, axis, distance):
    devices = range(lax.axis_size(axis))
    route = [(i - distance, i) for i in devices if i - distance in devices]
    return lax.ppermute(block, axis, route)


def tendency(center, east, west, upper, lower, wind_u, wind_v, damping, coupling):
    mixed = jnp.einsum("cd,mdlij->mclij", coupling, center, precision=lax.Precision.HIGHEST)
    advect = -wind_u * (east - west) * 0.5 - wind_v * (upper - lower) * 0.5
    return center + (advect + damping * (east + west + upper + lower - 4.0 * center) + mixed)


def lat_shifts(center):
    widths = ((0, 0),) * 4
    upper = jnp.pad(center[..., 1:], widths + ((0, 1),))
    lower = jnp.pad(center[..., :-1], widths + ((1, 0),))
    return (upper, lower)


def padded_step(padded, coefs, coupling):
    center = padded[:, :, :, 1:-1]
    east = padded[:, :, :, 2:]
    west = padded[:, :, :, :-2]
    upper, lower = lat_shifts(center)
    return tendency(center, east, west, upper, lower, coefs[0], coefs[1], coefs[2], coupling)


def per_device(forcing, trajectory, land_mask, coupling):
    own_forcing = forcing[0]
    damping = 0.15 * land_mask.astype(jnp.float32)
    coefs = jnp.concatenate([trajectory[0], damping[None]], axis=0)
    windows = lax.axis_size("tm")
    position = lax.axis_index("tm")
    state = own_forcing
    for hop in range(windows - 1):
        propagate_state = state
        for step in range(STEPS):
            padded = extended(propagate_state, (("space", 3),), 1)
            propagate_state = padded_step(padded, coefs, coupling)
        arrived = from_behind(propagate_state, "tm", 1)
        state = jnp.where(position == hop + 1, arrived + own_forcing, state)
    return state[None]


def solution(mesh):
    return jax.shard_map(
        per_device,
        mesh=mesh,
        in_specs=(
            P("tm", None, None, None, "space", None),
            P("tm", None, None, "space", None),
            P(None, "space", None),
            P(),
        ),
        out_specs=P("tm", None, None, None, "space", None),
        check_vma=False,
    )
```

profile of v0, /device:TPU:7, one launch (start us, length us, event | category | flops | bytes accessed | tf_op | source)
XLA Modules:
  0.0 54.7 jit_solution(2215128981341488815)
XLA Ops:
  0.0 0.0 copy-start
  0.0 2.2 %copy.11 = f32[1,4,4,8,4,640]{5,2,4,3,1,0:T(4,128)S(1)} copy(f32[1,4,4,8,4,640]{5,4,3,2,1,0:T(4,128)} %param.4) | data formatting | bytes 2621440 | tf_op args[0]
  2.2 0.0 copy-start.2
  2.2 0.0 copy-start.3
  2.2 0.1 fusion.9
  2.3 0.3 collective-permute-start
  2.6 3.0 %collective-permute-start.1 = (f32[4,4,8,1,640]{4,1,3,2,0:T(4,128)S(1)}, f32[4,4,8,1,640]{4,1,3,2,0:T(4,128)S(1)}, u32[]{:S(2)}, u32[]{:S(2)}) collective-permute-start(f32[4,4,8,1,640]{4,1,3,2,0:T(4,128)S(1)} %get-tuple-element.9), channel_id=1, source_target_pairs={{0,1},{1,2},{2,3},{3,4},{4,5},{5,6},{6,7},{7,8},{8,9},{9,10},{10,1... | collective-permute-start | bytes 983048 | tf_op jit(solution)/shard_map/ppermute | solution.py:16
  5.6 0.0 copy-done.2
  5.6 0.0 copy-done.3
  5.7 0.8 %fusion.10 = (f32[4,4,8,4,639]{4,1,3,2,0:T(4,128)S(1)}, f32[4,4,8,4,639]{4,1,3,2,0:T(4,128)S(1)}) fusion(f32[4,4,8,4,640]{4,1,3,2,0:T(4,128)S(1)} %bitcast.33), kind=kLoop, calls=%fused_computation.21 | loop fusion | bytes 5234688 | tf_op jit(solution)/shard_map/slice | solution.py:36
  6.5 6.3 %collective-permute-done = f32[4,4,8,1,640]{4,1,3,2,0:T(4,128)S(1)} collective-permute-done((f32[4,4,8,1,640]{4,1,3,2,0:T(4,128)S(1)}, f32[4,4,8,1,640]{4,1,3,2,0:T(4,128)S(1)}, u32[]{:S(2)}, u32[]{:S(2)}) %collective-permute-start) | collective-permute-done | bytes 327712 | tf_op jit(solution)/shard_map/ppermute | solution.py:17
  12.8 5.1 %collective-permute-done.1 = f32[4,4,8,1,640]{4,1,3,2,0:T(4,128)S(1)} collective-permute-done((f32[4,4,8,1,640]{4,1,3,2,0:T(4,128)S(1)}, f32[4,4,8,1,640]{4,1,3,2,0:T(4,128)S(1)}, u32[]{:S(2)}, u32[]{:S(2)}) %collective-permute-start.1) | collective-permute-done | bytes 327712 | tf_op jit(solution)/shard_map/ppermute | solution.py:16
  17.9 4.7 %fusion.3 = f32[4,4,8,4,640]{4,1,3,2,0:T(4,128)S(1)} fusion(f32[4,4,8,4,640]{4,1,3,2,0:T(4,128)S(1)} %bitcast.34, f32[4,4,8,4,639]{4,1,3,2,0:T(4,128)S(1)} %get-tuple-element.12, f32[4,4,8,4,639]{4,1,3,2,0:T(4,128)S(1)} %get-tuple-element.11, f32[4,4,8,1,640]{4,1,3,2,0:T(4,128)S(1)} %collective-permute-done, ...), kind=kOutput, calls=%fused_computation.6 | convolution fusion | flops 21626880 | bytes 6139968 | tf_op jit(solution)/shard_map/cd,mdlij->mclij/dot_general | solution.py:29
  22.6 0.1 fusion.7
  22.6 0.3 collective-permute-start.2
  23.0 3.0 %collective-permute-start.3 = (f32[4,4,8,1,640]{4,1,3,2,0:T(4,128)S(1)}, f32[4,4,8,1,640]{4,1,3,2,0:T(4,128)S(1)}, u32[]{:S(2)}, u32[]{:S(2)}) collective-permute-start(f32[4,4,8,1,640]{4,1,3,2,0:T(4,128)S(1)} %get-tuple-element.5), channel_id=1, source_target_pairs={{0,1},{1,2},{2,3},{3,4},{4,5},{5,6},{6,7},{7,8},{8,9},{9,10},{10,1... | collective-permute-start | bytes 983048 | tf_op jit(solution)/shard_map/ppermute | solution.py:16
  26.0 0.8 %fusion.8 = (f32[4,4,8,4,639]{4,1,3,2,0:T(4,128)S(1)}, f32[4,4,8,4,639]{4,1,3,2,0:T(4,128)S(1)}) fusion(f32[4,4,8,4,640]{4,1,3,2,0:T(4,128)S(1)} %fusion.3), kind=kLoop, calls=%fused_computation.19 | loop fusion | bytes 5234688 | tf_op jit(solution)/shard_map/slice | solution.py:36
  26.8 5.5 %collective-permute-done.2 = f32[4,4,8,1,640]{4,1,3,2,0:T(4,128)S(1)} collective-permute-done((f32[4,4,8,1,640]{4,1,3,2,0:T(4,128)S(1)}, f32[4,4,8,1,640]{4,1,3,2,0:T(4,128)S(1)}, u32[]{:S(2)}, u32[]{:S(2)}) %collective-permute-start.2) | collective-permute-done | bytes 327712 | tf_op jit(solution)/shard_map/ppermute | solution.py:17
  32.3 9.1 %collective-permute-done.3 = f32[4,4,8,1,640]{4,1,3,2,0:T(4,128)S(1)} collective-permute-done((f32[4,4,8,1,640]{4,1,3,2,0:T(4,128)S(1)}, f32[4,4,8,1,640]{4,1,3,2,0:T(4,128)S(1)}, u32[]{:S(2)}, u32[]{:S(2)}) %collective-permute-start.3) | collective-permute-done | bytes 327712 | tf_op jit(solution)/shard_map/ppermute | solution.py:16
  41.4 5.5 %fusion.1 = f32[4,4,8,4,640]{4,1,3,2,0:T(4,128)} fusion(f32[4,4,8,4,640]{4,1,3,2,0:T(4,128)S(1)} %fusion.3, f32[4,4,8,4,639]{4,1,3,2,0:T(4,128)S(1)} %get-tuple-element.8, f32[4,4,8,4,639]{4,1,3,2,0:T(4,128)S(1)} %get-tuple-element.7, f32[4,4,8,1,640]{4,1,3,2,0:T(4,128)S(1)} %collective-permute-done.2, f32[4,4,8,1,640]{4,1,3,2,0:T(4,128)S(1)} %collective-permute-done.3, ...), kind=kOutput, calls=%fused_computation.3 | convolution fusion | flops 21626880 | bytes 6139968 | tf_op jit(solution)/shard_map/cd,mdlij->mclij/dot_general | solution.py:29
  46.9 1.3 %collective-permute-start.4 = (f32[4,4,8,4,640]{4,1,3,2,0:T(4,128)}, f32[4,4,8,4,640]{4,1,3,2,0:T(4,128)S(1)}, u32[]{:S(2)}, u32[]{:S(2)}) collective-permute-start(f32[4,4,8,4,640]{4,1,3,2,0:T(4,128)} %fusion.1), channel_id=1, source_target_pairs={{0,16},{1,17},{2,18},{3,19},{4,20},{5,21},{6,22},{7,23},{8,24},{9,... | collective-permute-start | bytes 3932168 | tf_op jit(solution)/shard_map/ppermute | solution.py:25
  48.2 4.1 %collective-permute-done.4 = f32[4,4,8,4,640]{4,1,3,2,0:T(4,128)S(1)} collective-permute-done((f32[4,4,8,4,640]{4,1,3,2,0:T(4,128)}, f32[4,4,8,4,640]{4,1,3,2,0:T(4,128)S(1)}, u32[]{:S(2)}, u32[]{:S(2)}) %collective-permute-start.4) | collective-permute-done | bytes 1310752 | tf_op jit(solution)/shard_map/ppermute | solution.py:25
  52.2 1.0 %fusion.4 = f32[1,4,4,8,4,640]{5,2,4,3,1,0:T(4,128)S(1)} fusion(f32[4,4,8,4,640]{4,1,3,2,0:T(4,128)S(1)} %collective-permute-done.4, pred[]{:T(512)S(6)} %eq.3, f32[1,4,4,8,4,640]{5,4,3,2,1,0:T(4,128)S(1)} %copy-done.1), kind=kLoop, calls=%fused_computation.7 | loop fusion | flops 655360 | bytes 3932161 | tf_op jit(solution)/shard_map/broadcast_in_dim | solution.py:63
  53.3 1.4 %copy.6 = f32[1,4,4,8,4,640]{5,4,3,2,1,0:T(4,128)} copy(f32[1,4,4,8,4,640]{5,2,4,3,1,0:T(4,128)S(1)} %fusion.4) | data formatting | bytes 2621440 | tf_op jit(solution)/shard_map/broadcast_in_dim | solution.py:63
  (5 shorter events, 0.1 us)
Async XLA Ops:
  0.0 17.9 %copy-start = (f32[4,4]{1,0:T(4,128)S(1)}, f32[4,4]{1,0:T(4,128)}, u32[]{:S(2)}) copy-start(f32[4,4]{1,0:T(4,128)} %param.7) | copy-start | bytes 196
  2.2 3.4 %copy-start.2 = (f32[1,2,8,4,640]{4,3,2,1,0:T(4,128)S(1)}, f32[1,2,8,4,640]{4,3,2,1,0:T(4,128)}, u32[]{:S(2)}) copy-start(f32[1,2,8,4,640]{4,3,2,1,0:T(4,128)} %param.5) | copy-start | bytes 491524
  2.2 3.4 %copy-start.3 = (s32[8,4,640]{2,1,0:T(4,128)S(1)}, s32[8,4,640]{2,1,0:T(4,128)}, u32[]{:S(2)}) copy-start(s32[8,4,640]{2,1,0:T(4,128)} %param.6) | copy-start | bytes 245764
  2.3 10.5 %collective-permute-start = (f32[4,4,8,1,640]{4,1,3,2,0:T(4,128)S(1)}, f32[4,4,8,1,640]{4,1,3,2,0:T(4,128)S(1)}, u32[]{:S(2)}, u32[]{:S(2)}) collective-permute-start(f32[4,4,8,1,640]{4,1,3,2,0:T(4,128)S(1)} %get-tuple-element.10), channel_id=1, source_target_pairs={{1,0},{2,1},{3,2},{4,3},{5,4},{6,5},{7,6},{8,7},{9,8},{10,9},{11,1... | collective-permute-start | bytes 983048 | tf_op jit(solution)/shard_map/ppermute | solution.py:17
  2.6 15.3 %collective-permute-start.1 = (f32[4,4,8,1,640]{4,1,3,2,0:T(4,128)S(1)}, f32[4,4,8,1,640]{4,1,3,2,0:T(4,128)S(1)}, u32[]{:S(2)}, u32[]{:S(2)}) collective-permute-start(f32[4,4,8,1,640]{4,1,3,2,0:T(4,128)S(1)} %get-tuple-element.9), channel_id=1, source_target_pairs={{0,1},{1,2},{2,3},{3,4},{4,5},{5,6},{6,7},{7,8},{8,9},{9,10},{10,1... | collective-permute-start | bytes 983048 | tf_op jit(solution)/shard_map/ppermute | solution.py:16
  22.6 9.6 %collective-permute-start.2 = (f32[4,4,8,1,640]{4,1,3,2,0:T(4,128)S(1)}, f32[4,4,8,1,640]{4,1,3,2,0:T(4,128)S(1)}, u32[]{:S(2)}, u32[]{:S(2)}) collective-permute-start(f32[4,4,8,1,640]{4,1,3,2,0:T(4,128)S(1)} %get-tuple-element.6), channel_id=1, source_target_pairs={{1,0},{2,1},{3,2},{4,3},{5,4},{6,5},{7,6},{8,7},{9,8},{10,9},{11,1... | collective-permute-start | bytes 983048 | tf_op jit(solution)/shard_map/ppermute | solution.py:17
  23.0 18.4 %collective-permute-start.3 = (f32[4,4,8,1,640]{4,1,3,2,0:T(4,128)S(1)}, f32[4,4,8,1,640]{4,1,3,2,0:T(4,128)S(1)}, u32[]{:S(2)}, u32[]{:S(2)}) collective-permute-start(f32[4,4,8,1,640]{4,1,3,2,0:T(4,128)S(1)} %get-tuple-element.5), channel_id=1, source_target_pairs={{0,1},{1,2},{2,3},{3,4},{4,5},{5,6},{6,7},{7,8},{8,9},{9,10},{10,1... | collective-permute-start | bytes 983048 | tf_op jit(solution)/shard_map/ppermute | solution.py:16
  41.4 10.9 %copy-start.1 = (f32[1,4,4,8,4,640]{5,4,3,2,1,0:T(4,128)S(1)}, f32[1,4,4,8,4,640]{5,4,3,2,1,0:T(4,128)}, u32[]{:S(2)}) copy-start(f32[1,4,4,8,4,640]{5,4,3,2,1,0:T(4,128)} %param.4) | copy-start | bytes 3932164
  46.9 5.4 %collective-permute-start.4 = (f32[4,4,8,4,640]{4,1,3,2,0:T(4,128)}, f32[4,4,8,4,640]{4,1,3,2,0:T(4,128)S(1)}, u32[]{:S(2)}, u32[]{:S(2)}) collective-permute-start(f32[4,4,8,4,640]{4,1,3,2,0:T(4,128)} %fusion.1), channel_id=1, source_target_pairs={{0,16},{1,17},{2,18},{3,19},{4,20},{5,21},{6,22},{7,23},{8,24},{9,... | collective-permute-start | bytes 3932168 | tf_op jit(solution)/shard_map/ppermute | solution.py:25
where the time goes:
time: 54.8 us; the launch traced here: 54.7 us
  waiting for transfers between devices  30.1 us (55%)
  matrix products  10.2 us (19%)
  starting transfers between devices  7.91 us (14%)
  local copies, waits for them, and re-layouts  5.31 us (10%)
  other arithmetic  1.06 us (2%)
    ppermute x2, waiting for transfers between devices, extended(): before = lax.ppermute(last, axis, up)  14.2 us
    ppermute x2, waiting for transfers between devices, extended(): after = lax.ppermute(leading, axis, down)  11.8 us
    dot_general x2, matrix products, tendency(): jnp.einsum('cd,mdlij->mclij', coupling, center, precision=lax.Precision.H...  10.2 us
    ppermute x2, starting transfers between devices, extended(): before = lax.ppermute(last, axis, up)  5.99 us
    ppermute x1, waiting for transfers between devices, from_behind(): return lax.ppermute(block, axis, route)  4.06 us
    unnamed x9, local copies, waits for them, and re-layouts  2.2 us
    slice x2, local copies, waits for them, and re-layouts, lat_shifts(): upper = jnp.pad(center[..., 1:], widths + ((0, 1),))  1.57 us
    broadcast_in_dim x1, local copies, waits for them, and re-layouts, per_device(): return state[None]  1.42 us
  transfers between devices with their start and end apart: 5, of which 5 were waited for; matrix products, arithmetic and copies ran while one was open for 3% of the time, Pallas kernels for 0%

commit v1 on v0

v1 whole, which is shorter than its diff:
```python
import functools
import math

import jax
import jax.numpy as jnp
from jax import lax
from jax.experimental import pallas as pl
from jax.experimental.pallas import tpu as pltpu
from jax.sharding import PartitionSpec as P


STEPS = 2
HBM = pl.BlockSpec(memory_space=pltpu.HBM)
VMEM = pl.BlockSpec(memory_space=pltpu.VMEM)
SMEM = pl.BlockSpec(memory_space=pltpu.SMEM)


def run_copies(pairs, sem):
    copies = [pltpu.make_async_copy(src, dst, sem.at[i]) for i, (src, dst) in enumerate(pairs)]
    for copy in copies:
        copy.start()
    return copies


def wait_all(copies):
    for copy in copies:
        copy.wait()


def is_even():
    return lax.rem(lax.axis_index("space"), 2) == 0


def shifts(x):
    width = x.shape[-1]
    return pltpu.roll(x, width - 1, 1), pltpu.roll(x, 1, 1)


def stencil(u, v, mask):
    nu = 0.15 * mask.astype(jnp.float32)
    u, v = 0.5 * u, 0.5 * v
    lat = lax.broadcasted_iota(jnp.int32, u.shape, 1)
    north = jnp.where(lat == u.shape[1] - 1, 0.0, nu - v)
    south = jnp.where(lat == 0, 0.0, nu + v)
    return 1.0 - 4.0 * nu, nu - u, nu + u, north, south


def edges_kernel(hop, x, traj, mask, near, far, wind, open_, sem):
    last = x.shape[1] - 1
    rows, lev = x.shape[0], traj.shape[1]

    def send(j_near, j_far):
        copies = run_copies(
            [
                (x.at[:, j_near, :], near.at[0:rows, :]),
                (x.at[:, j_far, :], far.at[0:rows, :]),
                (traj.at[0, :, 0, :], wind.at[0]),
                (traj.at[0, :, last, :], wind.at[1]),
                (mask.at[:, 0, :], open_.at[0]),
                (mask.at[:, last, :], open_.at[1]),
            ],
            sem,
        )
        wait_all(copies[2:])
        for j, ref in ((j_near, near), (j_far, far)):
            side = 0 if j == 0 else 1
            nu = 0.15 * open_[side].astype(jnp.float32)
            half = 0.5 * wind[side]
            ref[rows : rows + lev, :] = nu + half if j == 0 else nu - half
        wait_all(copies[:2])

    @pl.when(lax.axis_index("tm") == hop)
    def _():
        even = is_even()
        pl.when(even)(lambda: send(last, 0))
        pl.when(jnp.logical_not(even))(lambda: send(0, last))


def load_coefs(traj, mask, wind, open_, sem):
    lon = mask.shape[1]
    pairs = []
    for j in range(lon):
        pairs.append((traj.at[0, :, j, :], wind.at[0, j]))
        pairs.append((traj.at[1, :, j, :], wind.at[1, j]))
        pairs.append((mask.at[:, j, :], open_.at[j]))
    return run_copies(pairs, sem)


def partial_kernel(hop, var, x, traj, mask, coupling, near, far, xs, wind, open_, sem_x, sem_c):
    lon = x.shape[1]
    rows, lev = x.shape[0], traj.shape[1]
    last = lon - 1

    @pl.when(lax.axis_index("tm") == hop)
    def _():
        loads = run_copies([(x.at[:, j, :], xs.at[j]) for j in range(lon)], sem_x)
        wait_all(load_coefs(traj, mask, wind, open_, sem_c))
        wait_all(loads)

        def send(j_near, j_far):
            for j, out in ((j_near, near), (j_far, far)):
                inner = 1 if j == 0 else last - 1
                mid, east, west, north, south = stencil(wind[0, j], wind[1, j], open_[j])
                side = east if j == 0 else west

                def member(m, carry):
                    base = pl.multiple_of(m * var * lev, lev)
                    block = [xs[j, pl.ds(base + d * lev, lev), :] for d in range(var)]
                    for c in range(var):
                        up, low = shifts(block[c])
                        total = mid * block[c] + side * xs[inner, pl.ds(base + c * lev, lev), :]
                        total += north * up + south * low
                        for d in range(var):
                            total += coupling[c, d] * block[d]
                        out[pl.ds(base + c * lev, lev), :] = total
                    return carry

                lax.fori_loop(0, rows // (var * lev), member, 0)

        even = is_even()
        pl.when(even)(lambda: send(last, 0))
        pl.when(jnp.logical_not(even))(lambda: send(0, last))


def main_kernel(
    hop, var, own, sent, traj, mask, coupling, near, far, z, edge,
    xs, ss, halo, coef, force, wind, open_, sem_o, sem_x, sem_c, sem_h,
):
    rows, lon = own.shape[0], own.shape[1]
    lev = traj.shape[1]
    last = lon - 1
    receiver = lax.axis_index("tm") == hop + 1

    @pl.when(jnp.logical_not(receiver))
    def _():
        wait_all(run_copies([(own.at[:, j, :], z.at[j]) for j in range(lon)], sem_o))

    @pl.when(receiver)
    def _():
        loads = run_copies([(sent.at[:, j, :], xs.at[j]) for j in range(lon)], sem_x)
        coefs = load_coefs(traj, mask, wind, open_, sem_c)
        forces = run_copies([(own.at[:, j, :], force.at[j]) for j in range(lon)], sem_o)
        even = is_even()

        @pl.when(even)
        def _():
            wait_all(run_copies([(far, halo.at[0]), (near, halo.at[1])], sem_h))

        @pl.when(jnp.logical_not(even))
        def _():
            wait_all(run_copies([(near, halo.at[0]), (far, halo.at[1])], sem_h))

        wait_all(coefs)
        for j in range(lon):
            for k, value in enumerate(stencil(wind[0, j], wind[1, j], open_[j])):
                coef[k, j] = value
        edge[0] = coef[2, 0]
        edge[1] = coef[1, last]
        wait_all(loads)
        wait_all(forces)

        def step(j, centre, east, west, skip_e=False, skip_w=False):
            block = [centre(d) for d in range(var)]
            for c in range(var):
                up, low = shifts(block[c])
                total = coef[0, j] * block[c] + coef[3, j] * up + coef[4, j] * low
                if not skip_e:
                    total += coef[1, j] * east(c)
                if not skip_w:
                    total += coef[2, j] * west(c)
                for d in range(var):
                    total += coupling[c, d] * block[d]
                yield c, total

        def member(m, carry):
            base = pl.multiple_of(m * var * lev, lev)

            def at(ref, j):
                return lambda d: ref[j, pl.ds(base + d * lev, lev), :]

            for j in range(lon):
                east = at(xs, j + 1) if j < last else at(halo, 1)
                west = at(xs, j - 1) if j > 0 else at(halo, 0)
                for c, total in step(j, at(xs, j), east, west):
                    ss[j, pl.ds(base + c * lev, lev), :] = total
            weight = (
                coef[2, 0] * halo[0, rows : rows + lev, :],
                coef[1, last] * halo[1, rows : rows + lev, :],
            )
            for j in range(lon):
                east = at(ss, j + 1) if j < last else None
                west = at(ss, j - 1) if j > 0 else None
                for c, total in step(j, at(ss, j), east, west, j == last, j == 0):
                    total += at(force, j)(c)
                    if j == 0:
                        total += weight[0] * at(xs, j)(c)
                    if j == last:
                        total += weight[1] * at(xs, j)(c)
                    z[j, pl.ds(base + c * lev, lev), :] = total
            return carry

        lax.fori_loop(0, rows // (var * lev), member, 0)


def finish_kernel(hop, near, far, z, edge, out, done, sem):
    lon, rows = z.shape[0], z.shape[1]
    lev = edge.shape[1]
    last = lon - 1
    receiver = lax.axis_index("tm") == hop + 1

    @pl.when(jnp.logical_not(receiver))
    def _():
        wait_all(run_copies([(z.at[j], out.at[:, j, :]) for j in range(lon)], sem))

    @pl.when(receiver)
    def _():
        even = is_even()

        def finish(j_near, j_far):
            copies = [pltpu.make_async_copy(z.at[j], out.at[:, j, :], sem.at[j]) for j in range(1, last)]
            for copy in copies:
                copy.start()
            for j, ref in ((j_near, near), (j_far, far)):
                side = 0 if j == 0 else 1
                for r in range(0, rows, lev):
                    done[side, r : r + lev, :] = z[j, r : r + lev, :] + edge[side] * ref[r : r + lev, :]
                copy = pltpu.make_async_copy(done.at[side], out.at[:, j, :], sem.at[j])
                copy.start()
                copies.append(copy)
            wait_all(copies)

        pl.when(even)(lambda: finish(last, 0))
        pl.when(jnp.logical_not(even))(lambda: finish(0, last))


def call(kernel, out_shape, in_specs, out_specs, scratch, semaphores):
    room = sum(4 * math.prod(ref.inner_aval.shape) for ref in scratch)
    return pl.pallas_call(
        kernel,
        out_shape=out_shape,
        in_specs=in_specs,
        out_specs=out_specs,
        scratch_shapes=scratch + [pltpu.SemaphoreType.DMA((count,)) for count in semaphores],
        compiler_params=pltpu.CompilerParams(vmem_limit_bytes=room + 2**22),
    )


def advance(hop, state, traj, land_mask, coupling, var):
    rows, lon, lat = state.shape
    lev = traj.shape[1]
    n = lax.axis_size("space")
    f32 = jnp.float32

    def buffer(*dims, dtype=f32):
        return pltpu.VMEM(dims, dtype)

    def moved(block, move):
        pairs = [(hop * n + s, (hop + 1) * n + move(s) % n) for s in range(n)]
        block = lax.ppermute(block, ("tm", "space"), pairs)
        return pltpu.with_memory_space_constraint(block, pltpu.VMEM)

    def to_near(s):
        return s + 1 if s % 2 == 0 else s - 1

    def to_far(s):
        return s - 1 if s % 2 == 0 else s + 1

    held = [pltpu.with_memory_space_constraint(a, pltpu.HBM) for a in (state, traj, land_mask)]
    near, far = call(
        functools.partial(edges_kernel, hop),
        [buffer(rows + lev, lat)] * 2,
        [HBM] * 3,
        [VMEM] * 2,
        [buffer(2, lev, lat), buffer(2, lev, lat, dtype=jnp.int32)],
        [6],
    )(*held)
    near_x = moved(near, to_near)
    far_x = moved(far, to_far)
    near, far = call(
        functools.partial(partial_kernel, hop, var),
        [buffer(rows, lat)] * 2,
        [HBM] * 3 + [SMEM],
        [VMEM] * 2,
        [buffer(lon, rows, lat), buffer(2, lon, lev, lat), buffer(lon, lev, lat, dtype=jnp.int32)],
        [lon, 3 * lon],
    )(*held, coupling)
    near_p = moved(near, to_near)
    far_p = moved(far, to_far)
    sent = moved(state, lambda s: s)
    sent_traj = moved(traj, lambda s: s)
    z, edge = call(
        functools.partial(main_kernel, hop, var),
        [buffer(lon, rows, lat), buffer(2, lev, lat)],
        [HBM, VMEM, VMEM, HBM, SMEM, VMEM, VMEM],
        [VMEM] * 2,
        [
            buffer(lon, rows, lat),
            buffer(lon, rows, lat),
            buffer(2, rows + lev, lat),
            buffer(5, lon, lev, lat),
            buffer(lon, rows, lat),
            buffer(2, lon, lev, lat),
            buffer(lon, lev, lat, dtype=jnp.int32),
        ],
        [lon, lon, 3 * lon, 2],
    )(held[0], sent, sent_traj, held[2], coupling, near_x, far_x)
    return call(
        functools.partial(finish_kernel, hop),
        jax.ShapeDtypeStruct(state.shape, f32),
        [VMEM] * 4,
        HBM,
        [buffer(2, rows, lat)],
        [lon],
    )(near_p, far_p, z, edge)


def per_device(forcing, trajectory, land_mask, coupling):
    _, mem, var, lev, lon, lat = forcing.shape
    assert lax.axis_size("space") % 2 == 0 and lon >= 2 and STEPS == 2
    state = forcing.reshape(mem * var * lev, lon, lat)
    for hop in range(lax.axis_size("tm") - 1):
        state = advance(hop, state, trajectory[0], land_mask, coupling, var)
    return state.reshape(forcing.shape)


def solution(mesh):
    return jax.shard_map(
        per_device,
        mesh=mesh,
        in_specs=(
            P("tm", None, None, None, "space", None),
            P("tm", None, None, "space", None),
            P(None, "space", None),
            P(),
        ),
        out_specs=P("tm", None, None, None, "space", None),
        check_vma=False,
    )
```

time: 54.8 us -> 27 us (0.49)
  the two profiles are of different devices: /device:TPU:7 before, /device:TPU:13 now
where the time goes in v1:
time: 27 us; the launch traced here: 26.7 us
  waiting for transfers between devices  11 us (41%)
  starting transfers between devices  7.87 us (29%)
  Pallas kernels  7.73 us (29%)
    ppermute x6, waiting for transfers between devices, moved(): block = lax.ppermute(block, ('tm', 'space'), pairs)  11 us
    ppermute x6, starting transfers between devices, moved(): block = lax.ppermute(block, ('tm', 'space'), pairs)  7.87 us
    pallas_call x1, Pallas kernels, advance(): call(functools.partial(main_kernel, hop, var), [buffer(lon, rows, lat), b...  5.81 us
    pallas_call x1, Pallas kernels, advance(): call(functools.partial(finish_kernel, hop), jax.ShapeDtypeStruct(state.sh...  1.13 us
    pallas_call x1, Pallas kernels, advance(): call(functools.partial(partial_kernel, hop, var), [buffer(rows, lat)] * 2...  0.73 us
  transfers between devices with their start and end apart: 6, of which 1 were waited for; matrix products, arithmetic and copies ran while one was open for 0% of the time, Pallas kernels for 25%

profile of v1, /device:TPU:13, one launch (start us, length us, event | category | flops | bytes accessed | tf_op | source)
XLA Modules:
  0.0 26.7 jit_solution(4928964953554182705)
XLA Ops:
  0.0 0.0 copy-start
  0.0 1.4 %collective-permute-start.2 = (f32[128,4,640]{2,1,0:T(4,128)}, f32[128,4,640]{2,1,0:T(4,128)S(1)}, u32[]{:S(2)}, u32[]{:S(2)}) collective-permute-start(f32[128,4,640]{2,1,0:T(4,128)} %bitcast.3), channel_id=1, source_target_pairs={{0,16},{1,17},{2,18},{3,19},{4,20},{5,21},{6,22},{7,23},{8,24},{9,... | collective-permute-start | bytes 3932168 | tf_op jit(solution)/shard_map/ppermute | solution.py:259
  1.4 1.3 %collective-permute-start.3 = (f32[2,8,4,640]{3,2,1,0:T(4,128)}, f32[2,8,4,640]{3,2,1,0:T(4,128)S(1)}, u32[]{:S(2)}, u32[]{:S(2)}) collective-permute-start(f32[2,8,4,640]{3,2,1,0:T(4,128)} %bitcast.7), channel_id=1, source_target_pairs={{0,16},{1,17},{2,18},{3,19},{4,20},{5,21},{6,22},{7,23},{8,24},{9,... | collective-permute-start | bytes 491528 | tf_op jit(solution)/shard_map/ppermute | solution.py:259
  2.7 0.1 shard_map.47
  2.8 1.3 %collective-permute-start.4 = (f32[136,640]{1,0:T(8,128)S(1)}, f32[136,640]{1,0:T(8,128)S(1)}, u32[]{:S(2)}, u32[]{:S(2)}) collective-permute-start(f32[136,640]{1,0:T(8,128)S(1)} %get-tuple-element.13), channel_id=1, source_target_pairs={{0,17},{1,16},{2,19},{3,18},{4,21},{5,20},{6,23},{7,22},{8,25},{9,... | collective-permute-start | bytes 1044488 | tf_op jit(solution)/shard_map/ppermute | solution.py:259
  4.1 1.3 %collective-permute-start.5 = (f32[136,640]{1,0:T(8,128)S(1)}, f32[136,640]{1,0:T(8,128)S(1)}, u32[]{:S(2)}, u32[]{:S(2)}) collective-permute-start(f32[136,640]{1,0:T(8,128)S(1)} %get-tuple-element.14), channel_id=1, source_target_pairs={{0,31},{1,18},{2,17},{3,20},{4,19},{5,22},{6,21},{7,24},{8,23},{9,... | collective-permute-start | bytes 1044488 | tf_op jit(solution)/shard_map/ppermute | solution.py:259
  5.4 0.0 copy-done
  5.4 0.7 %shard_map.46 = (f32[128,640]{1,0:T(8,128)S(1)}, f32[128,640]{1,0:T(8,128)S(1)}) custom-call(f32[128,4,640]{2,1,0:T(4,128)} %bitcast.5, f32[2,8,4,640]{3,2,1,0:T(4,128)} %bitcast.9, s32[8,4,640]{2,1,0:T(4,128)} %mask.5, f32[4,4]{1,0:T(4,128)S(1)} %copy-done), custom_call_target="tpu_custom_call" | custom-call | tf_op jit(solution)/shard_map/pallas_call | solution.py:279
  6.1 1.3 %collective-permute-start = (f32[128,640]{1,0:T(8,128)S(1)}, f32[128,640]{1,0:T(8,128)S(1)}, u32[]{:S(2)}, u32[]{:S(2)}) collective-permute-start(f32[128,640]{1,0:T(8,128)S(1)} %get-tuple-element.11), channel_id=1, source_target_pairs={{0,17},{1,16},{2,19},{3,18},{4,21},{5,20},{6,23},{7,22},{8,25},{9,... | collective-permute-start | bytes 983048 | tf_op jit(solution)/shard_map/ppermute | solution.py:259
  7.4 0.0 collective-permute-done.3.traj
  7.5 1.3 %collective-permute-start.1 = (f32[128,640]{1,0:T(8,128)S(1)}, f32[128,640]{1,0:T(8,128)S(1)}, u32[]{:S(2)}, u32[]{:S(2)}) collective-permute-start(f32[128,640]{1,0:T(8,128)S(1)} %get-tuple-element.12), channel_id=1, source_target_pairs={{0,31},{1,18},{2,17},{3,20},{4,19},{5,22},{6,21},{7,24},{8,23},{9,... | collective-permute-start | bytes 983048 | tf_op jit(solution)/shard_map/ppermute | solution.py:259
  8.8 11.0 %collective-permute-done.4.near = f32[136,640]{1,0:T(8,128)S(1)} collective-permute-done((f32[136,640]{1,0:T(8,128)S(1)}, f32[136,640]{1,0:T(8,128)S(1)}, u32[]{:S(2)}, u32[]{:S(2)}) %collective-permute-start.4) | collective-permute-done | bytes 348192 | tf_op jit(solution)/shard_map/ppermute | solution.py:259
  19.7 0.0 collective-permute-done.5.far
  19.7 0.0 collective-permute-done.2.sent
  19.7 5.8 %shard_map.48 = (f32[4,128,640]{2,1,0:T(8,128)S(1)}, f32[2,8,640]{2,1,0:T(8,128)S(1)}) custom-call(f32[128,4,640]{2,1,0:T(4,128)} %bitcast.6, f32[128,4,640]{2,1,0:T(4,128)S(1)} %collective-permute-done.2.sent, f32[2,8,4,640]{3,2,1,0:T(4,128)S(1)} %collective-permute-done.3.traj, s32[8,4,640]{2,1,0:T(4,128)} %mask.5, f32[4,4]{1,0:T(4,128)S(1)} %copy-done, ...), custom_call_target="tpu_custom_call" | custom-call | tf_op jit(solution)/shard_map/pallas_call | solution.py:291
  25.6 0.0 collective-permute-done.near
  25.6 0.0 collective-permute-done.1.far
  25.6 1.1 %shard_map.49 = f32[128,4,640]{2,1,0:T(4,128)} custom-call(f32[128,640]{1,0:T(8,128)S(1)} %collective-permute-done.near, f32[128,640]{1,0:T(8,128)S(1)} %collective-permute-done.1.far, f32[4,128,640]{2,1,0:T(8,128)S(1)} %get-tuple-element.15.z, f32[2,8,640]{2,1,0:T(8,128)S(1)} %get-tuple-element.16.edge), custom_call_target="tpu_custom_call" | custom-call | tf_op jit(solution)/shard_map/pallas_call | solution.py:307
Async XLA Ops:
  0.0 5.4 %copy-start = (f32[4,4]{1,0:T(4,128)S(1)}, f32[4,4]{1,0:T(4,128)}, u32[]{:S(2)}) copy-start(f32[4,4]{1,0:T(4,128)} %coupling.3) | copy-start | bytes 196
  0.0 19.7 %collective-permute-start.2 = (f32[128,4,640]{2,1,0:T(4,128)}, f32[128,4,640]{2,1,0:T(4,128)S(1)}, u32[]{:S(2)}, u32[]{:S(2)}) collective-permute-start(f32[128,4,640]{2,1,0:T(4,128)} %bitcast.3), channel_id=1, source_target_pairs={{0,16},{1,17},{2,18},{3,19},{4,20},{5,21},{6,22},{7,23},{8,24},{9,... | collective-permute-start | bytes 3932168 | tf_op jit(solution)/shard_map/ppermute | solution.py:259
  1.4 6.0 %collective-permute-start.3 = (f32[2,8,4,640]{3,2,1,0:T(4,128)}, f32[2,8,4,640]{3,2,1,0:T(4,128)S(1)}, u32[]{:S(2)}, u32[]{:S(2)}) collective-permute-start(f32[2,8,4,640]{3,2,1,0:T(4,128)} %bitcast.7), channel_id=1, source_target_pairs={{0,16},{1,17},{2,18},{3,19},{4,20},{5,21},{6,22},{7,23},{8,24},{9,... | collective-permute-start | bytes 491528 | tf_op jit(solution)/shard_map/ppermute | solution.py:259
  2.8 16.9 %collective-permute-start.4 = (f32[136,640]{1,0:T(8,128)S(1)}, f32[136,640]{1,0:T(8,128)S(1)}, u32[]{:S(2)}, u32[]{:S(2)}) collective-permute-start(f32[136,640]{1,0:T(8,128)S(1)} %get-tuple-element.13), channel_id=1, source_target_pairs={{0,17},{1,16},{2,19},{3,18},{4,21},{5,20},{6,23},{7,22},{8,25},{9,... | collective-permute-start | bytes 1044488 | tf_op jit(solution)/shard_map/ppermute | solution.py:259
  4.1 15.6 %collective-permute-start.5 = (f32[136,640]{1,0:T(8,128)S(1)}, f32[136,640]{1,0:T(8,128)S(1)}, u32[]{:S(2)}, u32[]{:S(2)}) collective-permute-start(f32[136,640]{1,0:T(8,128)S(1)} %get-tuple-element.14), channel_id=1, source_target_pairs={{0,31},{1,18},{2,17},{3,20},{4,19},{5,22},{6,21},{7,24},{8,23},{9,... | collective-permute-start | bytes 1044488 | tf_op jit(solution)/shard_map/ppermute | solution.py:259
  6.1 19.4 %collective-permute-start = (f32[128,640]{1,0:T(8,128)S(1)}, f32[128,640]{1,0:T(8,128)S(1)}, u32[]{:S(2)}, u32[]{:S(2)}) collective-permute-start(f32[128,640]{1,0:T(8,128)S(1)} %get-tuple-element.11), channel_id=1, source_target_pairs={{0,17},{1,16},{2,19},{3,18},{4,21},{5,20},{6,23},{7,22},{8,25},{9,... | collective-permute-start | bytes 983048 | tf_op jit(solution)/shard_map/ppermute | solution.py:259
  7.5 18.1 %collective-permute-start.1 = (f32[128,640]{1,0:T(8,128)S(1)}, f32[128,640]{1,0:T(8,128)S(1)}, u32[]{:S(2)}, u32[]{:S(2)}) collective-permute-start(f32[128,640]{1,0:T(8,128)S(1)} %get-tuple-element.12), channel_id=1, source_target_pairs={{0,31},{1,18},{2,17},{3,20},{4,19},{5,22},{6,21},{7,24},{8,23},{9,... | collective-permute-start | bytes 983048 | tf_op jit(solution)/shard_map/ppermute | solution.py:259

commit v2 on v0

v2 whole, which is shorter than its diff:
```python
import functools
import math

import jax
import jax.numpy as jnp
from jax import lax
from jax.experimental import pallas as pl
from jax.experimental.pallas import tpu as pltpu
from jax.sharding import PartitionSpec as P


STEPS = 2
HBM = pl.BlockSpec(memory_space=pltpu.HBM)
VMEM = pl.BlockSpec(memory_space=pltpu.VMEM)


def run_copies(pairs, sem):
    copies = [pltpu.make_async_copy(src, dst, sem.at[i]) for i, (src, dst) in enumerate(pairs)]
    for copy in copies:
        copy.start()
    return copies


def wait_all(copies):
    for copy in copies:
        copy.wait()


def by_parity(body, last):
    even = lax.rem(lax.axis_index("space"), 2) == 0
    pl.when(even)(lambda: body(last, 0))
    pl.when(jnp.logical_not(even))(lambda: body(0, last))


def shifts(x):
    return pltpu.roll(x, x.shape[-1] - 1, 1), pltpu.roll(x, 1, 1)


def stencil(u, v, nu):
    u, v = 0.5 * u, 0.5 * v
    lat = lax.broadcasted_iota(jnp.int32, u.shape, 1)
    north = jnp.where(lat == u.shape[1] - 1, 0.0, nu - v)
    south = jnp.where(lat == 0, 0.0, nu + v)
    return 1.0 - 4.0 * nu, nu - u, nu + u, north, south


def spread(coupling, shape):
    var = coupling.shape[0]
    table = coupling[...]
    return [[jnp.broadcast_to(table[c : c + 1, d : d + 1], shape) for d in range(var)] for c in range(var)]


def mix(pair, block, c):
    width = block[0].shape[1] // pair[c][0].shape[1]
    total = None
    for d, field in enumerate(block):
        term = jnp.tile(pair[c][d], (1, width)) * field
        total = term if total is None else total + term
    return total


class Packed:
    def __init__(self, ref, j, rows, lev):
        self.ref, self.j, self.rows, self.lev = ref, j, rows, lev

    def field(self, base):
        return self.ref[self.j, pl.ds(base, self.lev), :]

    def weights(self):
        u, v, nu = (self.ref[self.j, self.rows + k * self.lev : self.rows + (k + 1) * self.lev, :] for k in range(3))
        return stencil(u, v, nu)


def edges_kernel(hop, x, traj, mask, near, far, packed, open_, sem):
    rows, lon = x.shape[0], x.shape[1]
    lev = traj.shape[1]
    last = lon - 1

    @pl.when(lax.axis_index("tm") == hop)
    def _():
        fields = [(x.at[:, j, :], packed.at[j, 0:rows, :]) for j in (0, last, *range(1, last))]
        others = []
        for j in range(lon):
            for k in range(2):
                start = rows + k * lev
                others.append((traj.at[k, :, j, :], packed.at[j, start : start + lev, :]))
            others.append((mask.at[:, j, :], open_.at[j]))
        copies = run_copies(fields[:2] + others + fields[2:], sem)
        wait_all(copies[2 : 2 + len(others)])
        for j in range(lon):
            packed[j, rows + 2 * lev :, :] = 0.15 * open_[j].astype(jnp.float32)
        wait_all(copies[:2])

        def fill(j_near, j_far):
            for j, ref in ((j_near, near), (j_far, far)):
                _, east, west, _, _ = Packed(packed, j, rows, lev).weights()
                for r in range(0, rows, lev):
                    ref[r : r + lev, :] = packed[j, r : r + lev, :]
                ref[rows:, :] = west if j == 0 else east

        by_parity(fill, last)
        wait_all(copies[2 + len(others) :])


def partial_kernel(hop, packed, coupling, near, far):
    last = packed.shape[0] - 1
    rows, var = near.shape[0], coupling.shape[0]
    lev = (packed.shape[1] - rows) // 3

    @pl.when(lax.axis_index("tm") == hop)
    def _():
        pair = spread(coupling, (lev, 128))

        def send(j_near, j_far):
            for j, out in ((j_far, far), (j_near, near)):
                here = Packed(packed, j, rows, lev)
                inner = Packed(packed, 1 if j == 0 else last - 1, rows, lev)
                mid, east, west, north, south = here.weights()
                side = east if j == 0 else west

                def member(m, carry):
                    base = pl.multiple_of(m * var * lev, lev)
                    block = [here.field(base + d * lev) for d in range(var)]
                    for c in range(var):
                        up, low = shifts(block[c])
                        total = mid * block[c] + side * inner.field(base + c * lev)
                        total += north * up + south * low
                        out[pl.ds(base + c * lev, lev), :] = total + mix(pair, block, c)
                    return carry

                lax.fori_loop(0, rows // (var * lev), member, 0)

        by_parity(send, last)


def main_kernel(hop, own, packed, sent, coupling, near, far, out, z, edge, ss, halo, coef, force, sem_o, sem_h):
    rows, lon = own.shape[0], own.shape[1]
    var = coupling.shape[0]
    lev = (sent.shape[1] - rows) // 3
    last = lon - 1
    row = lax.axis_index("tm")

    @pl.when(row == hop)
    def _():
        wait_all(run_copies([(packed.at[j, 0:rows, :], out.at[:, j, :]) for j in range(lon)], sem_o))

    @pl.when(jnp.logical_and(row != hop, row != hop + 1))
    def _():
        wait_all(run_copies([(own.at[:, j, :], force.at[j]) for j in range(lon)], sem_o))
        wait_all(run_copies([(force.at[j], out.at[:, j, :]) for j in range(lon)], sem_o))

    @pl.when(row == hop + 1)
    def _():
        forces = run_copies([(own.at[:, j, :], force.at[j]) for j in range(lon)], sem_o)

        def fill(j_near, j_far):
            pairs = [(ref, halo.at[0 if j == 0 else 1]) for j, ref in ((j_near, near), (j_far, far))]
            wait_all(run_copies(pairs, sem_h))

        by_parity(fill, last)
        for j in range(lon):
            for k, value in enumerate(Packed(sent, j, rows, lev).weights()):
                coef[k, j] = value
        edge[0] = coef[2, 0]
        edge[1] = coef[1, last]
        pair = spread(coupling, (lev, 128))

        def at(ref, j, base):
            return lambda d: ref[j, pl.ds(base + d * lev, lev), :]

        def step(j, centre, east, west):
            block = [centre(d) for d in range(var)]
            for c in range(var):
                up, low = shifts(block[c])
                total = coef[0, j] * block[c] + coef[3, j] * up + coef[4, j] * low
                if east is not None:
                    total += coef[1, j] * east(c)
                if west is not None:
                    total += coef[2, j] * west(c)
                yield c, total + mix(pair, block, c)

        def first(m, carry):
            base = pl.multiple_of(m * var * lev, lev)
            for j in range(lon):
                east = at(sent, j + 1, base) if j < last else at(halo, 1, base)
                west = at(sent, j - 1, base) if j > 0 else at(halo, 0, base)
                for c, total in step(j, at(sent, j, base), east, west):
                    ss[j, pl.ds(base + c * lev, lev), :] = total
            return carry

        members = rows // (var * lev)
        lax.fori_loop(0, members, first, 0)
        wait_all(forces)

        def second(m, carry):
            base = pl.multiple_of(m * var * lev, lev)
            weight = {0: coef[2, 0] * halo[0, rows:, :], last: coef[1, last] * halo[1, rows:, :]}
            for j in range(lon):
                east = at(ss, j + 1, base) if j < last else None
                west = at(ss, j - 1, base) if j > 0 else None
                for c, total in step(j, at(ss, j, base), east, west):
                    total += at(force, j, base)(c)
                    if j in weight:
                        total += weight[j] * at(sent, j, base)(c)
                    z[j, pl.ds(base + c * lev, lev), :] = total
            return carry

        lax.fori_loop(0, members, second, 0)


def finish_kernel(hop, whole, block, z, edge, out_in, out, done, sem):
    del out_in
    lon, rows = z.shape[0], z.shape[1]
    lev = edge.shape[1]
    last = lon - 1

    @pl.when(lax.axis_index("tm") == hop + 1)
    def _():
        copies = []
        if whole:
            copies = run_copies([(z.at[j], out.at[:, j, :]) for j in range(1, last)], sem)

        def finish(j_near, j_far):
            j = j_far if whole else j_near
            weight = edge[0 if j == 0 else 1]
            for r in range(0, rows, lev):
                done[r : r + lev, :] = z[j, r : r + lev, :] + weight * block[r : r + lev, :]
            copy = pltpu.make_async_copy(done, out.at[:, j, :], sem.at[last])
            copy.start()
            copy.wait()

        by_parity(finish, last)
        wait_all(copies)


def call(kernel, out_shape, in_specs, out_specs, scratch, semaphores, aliases=None):
    room = sum(4 * math.prod(ref.inner_aval.shape) for ref in scratch)
    return pl.pallas_call(
        kernel,
        out_shape=out_shape,
        in_specs=in_specs,
        out_specs=out_specs,
        scratch_shapes=scratch + [pltpu.SemaphoreType.DMA((count,)) for count in semaphores],
        compiler_params=pltpu.CompilerParams(vmem_limit_bytes=room + 2**22),
        input_output_aliases=aliases or {},
    )


def advance(hop, state, traj, land_mask, coupling):
    rows, lon, lat = state.shape
    lev = traj.shape[1]
    n = lax.axis_size("space")
    f32 = jnp.float32

    def buffer(*dims, dtype=f32):
        return pltpu.VMEM(dims, dtype)

    def in_vmem(array):
        return pltpu.with_memory_space_constraint(array, pltpu.VMEM)

    def in_hbm(array):
        return pltpu.with_memory_space_constraint(array, pltpu.HBM)

    def moved(block, move):
        pairs = [(hop * n + s, (hop + 1) * n + move(s) % n) for s in range(n)]
        block = lax.ppermute(block, ("tm", "space"), pairs)
        return in_vmem(block)

    def to_near(s):
        return s + 1 if s % 2 == 0 else s - 1

    def to_far(s):
        return s - 1 if s % 2 == 0 else s + 1

    coupling = in_vmem(coupling)
    near, far, packed = call(
        functools.partial(edges_kernel, hop),
        [buffer(rows + lev, lat)] * 2 + [buffer(lon, rows + 3 * lev, lat)],
        [HBM] * 3,
        [VMEM] * 3,
        [buffer(lon, lev, lat, dtype=jnp.int32)],
        [4 * lon],
    )(in_hbm(state), in_hbm(traj), in_hbm(land_mask))
    near_x = moved(near, to_near)
    far_x = moved(far, to_far)
    sent = moved(packed, lambda s: s)
    packed = in_vmem(packed)
    near, far = call(
        functools.partial(partial_kernel, hop),
        [buffer(rows, lat)] * 2,
        [VMEM] * 2,
        [VMEM] * 2,
        [],
        [],
    )(packed, coupling)
    far_p = moved(far, to_far)
    near_p = moved(near, to_near)
    out = jax.ShapeDtypeStruct(state.shape, f32)
    state, z, edge = call(
        functools.partial(main_kernel, hop),
        [out, buffer(lon, rows, lat), buffer(2, lev, lat)],
        [HBM] + [VMEM] * 5,
        [HBM] + [VMEM] * 2,
        [
            buffer(lon, rows, lat),
            buffer(2, rows + lev, lat),
            buffer(5, lon, lev, lat),
            buffer(lon, rows, lat),
        ],
        [lon, 2],
    )(in_hbm(state), packed, sent, coupling, near_x, far_x)
    z, edge = in_vmem(z), in_vmem(edge)
    for whole, block in ((True, far_p), (False, near_p)):
        state = call(
            functools.partial(finish_kernel, hop, whole),
            out,
            [VMEM] * 3 + [HBM],
            HBM,
            [buffer(rows, lat)],
            [lon],
            {3: 0},
        )(block, z, edge, in_hbm(state))
    return state


def per_device(forcing, trajectory, land_mask, coupling):
    _, mem, var, lev, lon, lat = forcing.shape
    assert lax.axis_size("space") % 2 == 0 and lon >= 2 and STEPS == 2
    state = forcing.reshape(mem * var * lev, lon, lat)
    for hop in range(lax.axis_size("tm") - 1):
        state = advance(hop, state, trajectory[0], land_mask, coupling)
    return state.reshape(forcing.shape)


def solution(mesh):
    return jax.shard_map(
        per_device,
        mesh=mesh,
        in_specs=(
            P("tm", None, None, None, "space", None),
            P("tm", None, None, "space", None),
            P(None, "space", None),
            P(),
        ),
        out_specs=P("tm", None, None, None, "space", None),
        check_vma=False,
    )
```

time: 54.8 us -> 23.7 us (0.43)
  the two profiles are of different devices: /device:TPU:7 before, /device:TPU:1 now
where the time goes in v2:
time: 23.7 us; the launch traced here: 23.4 us
  waiting for transfers between devices  12.1 us (51%)
  starting transfers between devices  6.46 us (27%)
  Pallas kernels  4.78 us (20%)
    ppermute x5, waiting for transfers between devices, moved(): block = lax.ppermute(block, ('tm', 'space'), pairs)  12.1 us
    ppermute x5, starting transfers between devices, moved(): block = lax.ppermute(block, ('tm', 'space'), pairs)  6.46 us
    pallas_call x1, Pallas kernels, advance(): call(functools.partial(main_kernel, hop), [out, buffer(lon, rows, lat), b...  2.85 us
    pallas_call x2, Pallas kernels, advance(): call(functools.partial(finish_kernel, hop, whole), out, [VMEM] * 3 + [HBM...  1.77 us
  transfers between devices with their start and end apart: 5, of which 4 were waited for; matrix products, arithmetic and copies ran while one was open for 0% of the time, Pallas kernels for 16%

profile of v2, /device:TPU:1, one launch (start us, length us, event | category | flops | bytes accessed | tf_op | source)
XLA Modules:
  0.0 23.4 jit_solution(15841741286530848746)
XLA Ops:
  0.0 0.0 copy-start
  0.0 0.1 shard_map.46
  0.2 1.3 %collective-permute-start.1 = (f32[4,152,640]{2,1,0:T(8,128)S(1)}, f32[4,152,640]{2,1,0:T(8,128)S(1)}, u32[]{:S(2)}, u32[]{:S(2)}) collective-permute-start(f32[4,152,640]{2,1,0:T(8,128)S(1)} %get-tuple-element.13.packed), channel_id=1, source_target_pairs={{0,16},{1,17},{2,18},{3,19},{4,20},{5,21},{6,22},{7,23},{8,24},{9,... | collective-permute-start | bytes 4669448 | tf_op jit(solution)/shard_map/ppermute | solution.py:266
  1.5 1.3 %collective-permute-start.2 = (f32[136,640]{1,0:T(8,128)S(1)}, f32[136,640]{1,0:T(8,128)S(1)}, u32[]{:S(2)}, u32[]{:S(2)}) collective-permute-start(f32[136,640]{1,0:T(8,128)S(1)} %get-tuple-element.15), channel_id=1, source_target_pairs={{0,17},{1,16},{2,19},{3,18},{4,21},{5,20},{6,23},{7,22},{8,25},{9,... | collective-permute-start | bytes 1044488 | tf_op jit(solution)/shard_map/ppermute | solution.py:266
  2.8 1.3 %collective-permute-start.3 = (f32[136,640]{1,0:T(8,128)S(1)}, f32[136,640]{1,0:T(8,128)S(1)}, u32[]{:S(2)}, u32[]{:S(2)}) collective-permute-start(f32[136,640]{1,0:T(8,128)S(1)} %get-tuple-element.16), channel_id=1, source_target_pairs={{0,31},{1,18},{2,17},{3,20},{4,19},{5,22},{6,21},{7,24},{8,23},{9,... | collective-permute-start | bytes 1044488 | tf_op jit(solution)/shard_map/ppermute | solution.py:266
  4.1 0.0 copy-done
  4.1 1.3 %collective-permute-start.4 = (f32[128,640]{1,0:T(8,128)S(1)}, f32[128,640]{1,0:T(8,128)S(1)}, u32[]{:S(2)}, u32[]{:S(2)}) collective-permute-start(f32[128,640]{1,0:T(8,128)S(1)} %get-tuple-element.19), channel_id=1, source_target_pairs={{0,31},{1,18},{2,17},{3,20},{4,19},{5,22},{6,21},{7,24},{8,23},{9,... | collective-permute-start | bytes 983048 | tf_op jit(solution)/shard_map/ppermute | solution.py:266
  5.4 1.3 %collective-permute-start = (f32[128,640]{1,0:T(8,128)S(1)}, f32[128,640]{1,0:T(8,128)S(1)}, u32[]{:S(2)}, u32[]{:S(2)}) collective-permute-start(f32[128,640]{1,0:T(8,128)S(1)} %get-tuple-element.14), channel_id=1, source_target_pairs={{0,17},{1,16},{2,19},{3,18},{4,21},{5,20},{6,23},{7,22},{8,25},{9,... | collective-permute-start | bytes 983048 | tf_op jit(solution)/shard_map/ppermute | solution.py:266
  6.7 5.2 %collective-permute-done.2.near = f32[136,640]{1,0:T(8,128)S(1)} collective-permute-done((f32[136,640]{1,0:T(8,128)S(1)}, f32[136,640]{1,0:T(8,128)S(1)}, u32[]{:S(2)}, u32[]{:S(2)}) %collective-permute-start.2) | collective-permute-done | bytes 348192 | tf_op jit(solution)/shard_map/ppermute | solution.py:266
  11.9 5.4 %collective-permute-done.3.far = f32[136,640]{1,0:T(8,128)S(1)} collective-permute-done((f32[136,640]{1,0:T(8,128)S(1)}, f32[136,640]{1,0:T(8,128)S(1)}, u32[]{:S(2)}, u32[]{:S(2)}) %collective-permute-start.3) | collective-permute-done | bytes 348192 | tf_op jit(solution)/shard_map/ppermute | solution.py:266
  17.3 0.0 collective-permute-done.1.sent
  17.3 2.9 %shard_map.48 = (f32[128,4,640]{2,1,0:T(4,128)}, f32[4,128,640]{2,1,0:T(8,128)S(1)}, f32[2,8,640]{2,1,0:T(8,128)S(1)}) custom-call(f32[128,4,640]{2,1,0:T(4,128)} %bitcast.4, f32[4,152,640]{2,1,0:T(8,128)S(1)} %get-tuple-element.13.packed, f32[4,152,640]{2,1,0:T(8,128)S(1)} %collective-permute-done.1.sent, f32[4,4]{1,0:T(4,128)S(1)} %copy-done, ...), custom_call_target="tpu_custom_call" | custom-call | tf_op jit(solution)/shard_map/pallas_call | solution.py:299
  20.2 0.6 %collective-permute-done.4.block = f32[128,640]{1,0:T(8,128)S(1)} collective-permute-done((f32[128,640]{1,0:T(8,128)S(1)}, f32[128,640]{1,0:T(8,128)S(1)}, u32[]{:S(2)}, u32[]{:S(2)}) %collective-permute-start.4) | collective-permute-done | bytes 327712 | tf_op jit(solution)/shard_map/ppermute | solution.py:266
  20.8 1.0 %shard_map.49.out_in = f32[128,4,640]{2,1,0:T(4,128)} custom-call(f32[128,640]{1,0:T(8,128)S(1)} %collective-permute-done.4.block, f32[4,128,640]{2,1,0:T(8,128)S(1)} %get-tuple-element.17.z, f32[2,8,640]{2,1,0:T(8,128)S(1)} %get-tuple-element.18.edge, f32[128,4,640]{2,1,0:T(4,128)} %get-tuple-element.20.out_in), custom_call_target="tpu_custom_call", output_to_operand_aliasing={{}: (3, {})} | custom-call | tf_op jit(solution)/shard_map/pallas_call | solution.py:314
  21.8 0.8 %collective-permute-done.block = f32[128,640]{1,0:T(8,128)S(1)} collective-permute-done((f32[128,640]{1,0:T(8,128)S(1)}, f32[128,640]{1,0:T(8,128)S(1)}, u32[]{:S(2)}, u32[]{:S(2)}) %collective-permute-start) | collective-permute-done | bytes 327712 | tf_op jit(solution)/shard_map/ppermute | solution.py:266
  22.7 0.8 %shard_map.50 = f32[128,4,640]{2,1,0:T(4,128)} custom-call(f32[128,640]{1,0:T(8,128)S(1)} %collective-permute-done.block, f32[4,128,640]{2,1,0:T(8,128)S(1)} %get-tuple-element.17.z, f32[2,8,640]{2,1,0:T(8,128)S(1)} %get-tuple-element.18.edge, f32[128,4,640]{2,1,0:T(4,128)} %shard_map.49.out_in), custom_call_target="tpu_custom_call", output_to_operand_aliasing={{}: (3, {})} | custom-call | tf_op jit(solution)/shard_map/pallas_call | solution.py:314
  (1 shorter events, 0.0 us)
Async XLA Ops:
  0.0 4.1 %copy-start = (f32[4,4]{1,0:T(4,128)S(1)}, f32[4,4]{1,0:T(4,128)}, u32[]{:S(2)}) copy-start(f32[4,4]{1,0:T(4,128)} %coupling.3) | copy-start | bytes 196
  0.2 17.2 %collective-permute-start.1 = (f32[4,152,640]{2,1,0:T(8,128)S(1)}, f32[4,152,640]{2,1,0:T(8,128)S(1)}, u32[]{:S(2)}, u32[]{:S(2)}) collective-permute-start(f32[4,152,640]{2,1,0:T(8,128)S(1)} %get-tuple-element.13.packed), channel_id=1, source_target_pairs={{0,16},{1,17},{2,18},{3,19},{4,20},{5,21},{6,22},{7,23},{8,24},{9,... | collective-permute-start | bytes 4669448 | tf_op jit(solution)/shard_map/ppermute | solution.py:266
  1.5 10.4 %collective-permute-start.2 = (f32[136,640]{1,0:T(8,128)S(1)}, f32[136,640]{1,0:T(8,128)S(1)}, u32[]{:S(2)}, u32[]{:S(2)}) collective-permute-start(f32[136,640]{1,0:T(8,128)S(1)} %get-tuple-element.15), channel_id=1, source_target_pairs={{0,17},{1,16},{2,19},{3,18},{4,21},{5,20},{6,23},{7,22},{8,25},{9,... | collective-permute-start | bytes 1044488 | tf_op jit(solution)/shard_map/ppermute | solution.py:266
  2.8 14.6 %collective-permute-start.3 = (f32[136,640]{1,0:T(8,128)S(1)}, f32[136,640]{1,0:T(8,128)S(1)}, u32[]{:S(2)}, u32[]{:S(2)}) collective-permute-start(f32[136,640]{1,0:T(8,128)S(1)} %get-tuple-element.16), channel_id=1, source_target_pairs={{0,31},{1,18},{2,17},{3,20},{4,19},{5,22},{6,21},{7,24},{8,23},{9,... | collective-permute-start | bytes 1044488 | tf_op jit(solution)/shard_map/ppermute | solution.py:266
  4.1 16.7 %collective-permute-start.4 = (f32[128,640]{1,0:T(8,128)S(1)}, f32[128,640]{1,0:T(8,128)S(1)}, u32[]{:S(2)}, u32[]{:S(2)}) collective-permute-start(f32[128,640]{1,0:T(8,128)S(1)} %get-tuple-element.19), channel_id=1, source_target_pairs={{0,31},{1,18},{2,17},{3,20},{4,19},{5,22},{6,21},{7,24},{8,23},{9,... | collective-permute-start | bytes 983048 | tf_op jit(solution)/shard_map/ppermute | solution.py:266
  5.4 17.3 %collective-permute-start = (f32[128,640]{1,0:T(8,128)S(1)}, f32[128,640]{1,0:T(8,128)S(1)}, u32[]{:S(2)}, u32[]{:S(2)}) collective-permute-start(f32[128,640]{1,0:T(8,128)S(1)} %get-tuple-element.14), channel_id=1, source_target_pairs={{0,17},{1,16},{2,19},{3,18},{4,21},{5,20},{6,23},{7,22},{8,25},{9,... | collective-permute-start | bytes 983048 | tf_op jit(solution)/shard_map/ppermute | solution.py:266

commit v3 on v2

v3 whole, which is shorter than its diff:
```python
import functools
import math

import jax
import jax.numpy as jnp
from jax import lax
from jax.experimental import pallas as pl
from jax.experimental.pallas import tpu as pltpu
from jax.sharding import PartitionSpec as P


STEPS = 2
HBM = pl.BlockSpec(memory_space=pltpu.HBM)
VMEM = pl.BlockSpec(memory_space=pltpu.VMEM)


def run_copies(pairs, sem):
    copies = [pltpu.make_async_copy(src, dst, sem.at[i]) for i, (src, dst) in enumerate(pairs)]
    for copy in copies:
        copy.start()
    return copies


def wait_all(copies):
    for copy in copies:
        copy.wait()


def by_parity(body, last):
    even = lax.rem(lax.axis_index("space"), 2) == 0
    pl.when(even)(lambda: body(last, 0))
    pl.when(jnp.logical_not(even))(lambda: body(0, last))


def shifts(x):
    return pltpu.roll(x, x.shape[-1] - 1, 1), pltpu.roll(x, 1, 1)


def stencil(u, v, nu):
    u, v = 0.5 * u, 0.5 * v
    lat = lax.broadcasted_iota(jnp.int32, u.shape, 1)
    north = jnp.where(lat == u.shape[1] - 1, 0.0, nu - v)
    south = jnp.where(lat == 0, 0.0, nu + v)
    return 1.0 - 4.0 * nu, nu - u, nu + u, north, south


def spread(coupling, shape):
    var = coupling.shape[0]
    table = coupling[...]
    return [[jnp.broadcast_to(table[c : c + 1, d : d + 1], shape) for d in range(var)] for c in range(var)]


def mix(pair, block, c):
    width = block[0].shape[1] // pair[c][0].shape[1]
    total = None
    for d, field in enumerate(block):
        term = jnp.tile(pair[c][d], (1, width)) * field
        total = term if total is None else total + term
    return total


class Packed:
    def __init__(self, ref, j, rows, lev):
        self.ref, self.j, self.rows, self.lev = ref, j, rows, lev

    def field(self, base):
        return self.ref[self.j, pl.ds(base, self.lev), :]

    def weights(self):
        u, v, nu = (self.ref[self.j, self.rows + k * self.lev : self.rows + (k + 1) * self.lev, :] for k in range(3))
        return stencil(u, v, nu)


def edges_kernel(hop, x, traj, mask, near, far, wind, open_, sem):
    rows = x.shape[0]
    last = x.shape[1] - 1

    @pl.when(lax.axis_index("tm") == hop)
    def _():
        others = []
        for i, j in enumerate((0, last)):
            others.append((traj.at[0, :, j, :], wind.at[i]))
            others.append((mask.at[:, j, :], open_.at[i]))

        def fill(j_near, j_far):
            fields = [(x.at[:, j, :], ref.at[0:rows, :]) for j, ref in ((j_near, near), (j_far, far))]
            copies = run_copies(others + fields, sem)
            wait_all(copies[: len(others)])
            for j, ref in ((j_near, near), (j_far, far)):
                i = 0 if j == 0 else 1
                nu, half = 0.15 * open_[i].astype(jnp.float32), 0.5 * wind[i]
                ref[rows:, :] = nu + half if j == 0 else nu - half
            wait_all(copies[len(others) :])

        by_parity(fill, last)


def pack_kernel(hop, x, traj, mask, near, far, packed, open_, sem):
    rows, lon = x.shape[0], x.shape[1]
    lev = traj.shape[1]
    last = lon - 1

    @pl.when(lax.axis_index("tm") == hop)
    def _():
        pairs = []
        for j in range(lon):
            pairs.append((mask.at[:, j, :], open_.at[j]))
        for j in range(lon):
            for k in range(2):
                start = rows + k * lev
                pairs.append((traj.at[k, :, j, :], packed.at[j, start : start + lev, :]))
        pairs += [(x.at[:, j, :], packed.at[j, 0:rows, :]) for j in range(1, last)]
        copies = run_copies(pairs, sem)

        def fill(j_near, j_far):
            for j, ref in ((j_near, near), (j_far, far)):
                for r in range(0, rows, lev):
                    packed[j, r : r + lev, :] = ref[r : r + lev, :]

        by_parity(fill, last)
        wait_all(copies[:lon])
        for j in range(lon):
            packed[j, rows + 2 * lev :, :] = 0.15 * open_[j].astype(jnp.float32)
        wait_all(copies[lon:])


def partial_kernel(hop, to_far, packed, coupling, out):
    last = packed.shape[0] - 1
    rows, var = out.shape[0], coupling.shape[0]
    lev = (packed.shape[1] - rows) // 3

    @pl.when(lax.axis_index("tm") == hop)
    def _():
        pair = spread(coupling, (lev, 128))

        def send(j_near, j_far):
            j = j_far if to_far else j_near
            here = Packed(packed, j, rows, lev)
            inner = Packed(packed, 1 if j == 0 else last - 1, rows, lev)
            mid, east, west, north, south = here.weights()
            side = east if j == 0 else west

            def member(m, carry):
                base = pl.multiple_of(m * var * lev, lev)
                block = [here.field(base + d * lev) for d in range(var)]
                for c in range(var):
                    up, low = shifts(block[c])
                    total = mid * block[c] + side * inner.field(base + c * lev)
                    total += north * up + south * low
                    out[pl.ds(base + c * lev, lev), :] = total + mix(pair, block, c)
                return carry

            lax.fori_loop(0, rows // (var * lev), member, 0)

        by_parity(send, last)


def step(coef, coupling, j, centre, east, west):
    block = [centre(d) for d in range(len(coupling))]
    for c, field in enumerate(block):
        up, low = shifts(field)
        total = coef[0, j] * field + coef[3, j] * up + coef[4, j] * low
        if east is not None:
            total += coef[1, j] * east(c)
        if west is not None:
            total += coef[2, j] * west(c)
        yield c, total + mix(coupling, block, c)


def reader(ref, base, lev, *index):
    return lambda d: ref[(*index, pl.ds(base + d * lev, lev), slice(None))]


def main_kernel(hop, own, sent, coupling, z, coef, ss, sem):
    rows, lon = own.shape[0], own.shape[1]
    var = coupling.shape[0]
    lev = (sent.shape[1] - rows) // 3
    members = rows // (var * lev)

    @pl.when(lax.axis_index("tm") == hop + 1)
    def _():
        forces = run_copies([(own.at[:, j, :], z.at[j]) for j in range(lon)], sem)
        for j in range(lon):
            for k, value in enumerate(Packed(sent, j, rows, lev).weights()):
                coef[k, j] = value
        pair = spread(coupling, (lev, 128))

        def steps(ref, base):
            fields = {j: reader(ref, base, lev, j) for j in range(lon)}
            for j in range(lon):
                for c, total in step(coef, pair, j, fields[j], fields.get(j + 1), fields.get(j - 1)):
                    yield j, pl.ds(base + c * lev, lev), total

        def first(m, carry):
            for j, at, total in steps(sent, pl.multiple_of(m * var * lev, lev)):
                ss[j, at, :] = total
            return carry

        def second(m, carry):
            for j, at, total in steps(ss, pl.multiple_of(m * var * lev, lev)):
                z[j, at, :] += total
            return carry

        lax.fori_loop(0, members, first, 0)
        wait_all(forces)
        lax.fori_loop(0, members, second, 0)


def sides_kernel(hop, own, packed, sent, coupling, near, far, z, coef, out, ze, inner, sem):
    rows, lon = own.shape[0], own.shape[1]
    var = coupling.shape[0]
    lev = coef.shape[2]
    last = lon - 1
    members = rows // (var * lev)
    row = lax.axis_index("tm")

    @pl.when(row == hop)
    def _():
        wait_all(run_copies([(packed.at[j, 0:rows, :], out.at[:, j, :]) for j in range(lon)], sem))

    @pl.when(jnp.logical_and(row != hop, row != hop + 1))
    def _():
        for j in range(lon):
            wait_all(run_copies([(own.at[:, j, :], inner.at[0])], sem))
            wait_all(run_copies([(inner.at[0], out.at[:, j, :])], sem))

    @pl.when(row == hop + 1)
    def _():
        pair = spread(coupling, (lev, 128))

        def body(j_near, j_far):
            edges = {j_near: near, j_far: far}

            def added(j, base):
                weight = coef[2 if j == 0 else 1, j]
                return lambda d: weight * edges[j][pl.ds(base + d * lev, lev), :]

            def between(m, carry):
                base = pl.multiple_of(m * var * lev, lev)
                for j in range(1, last):
                    for c in range(var):
                        at = pl.ds(base + c * lev, lev)
                        total = z[j, at, :]
                        if j == 1:
                            total += coef[2, j] * added(0, base)(c)
                        if j == last - 1:
                            total += coef[1, j] * added(last, base)(c)
                        inner[j - 1, at, :] = total
                return carry

            lax.fori_loop(0, members, between, 0)
            copies = run_copies([(inner.at[j - 1], out.at[:, j, :]) for j in range(1, last)], sem)

            def outermost(m, carry):
                base = pl.multiple_of(m * var * lev, lev)
                for i, j in enumerate((0, last)):
                    weight = coef[2 if j == 0 else 1, j] * edges[j][rows:, :]
                    for c, total in step(coef, pair, j, added(j, base), None, None):
                        at = pl.ds(base + c * lev, lev)
                        ze[i, at, :] = z[j, at, :] + total + weight * sent[j, at, :]
                return carry

            lax.fori_loop(0, members, outermost, 0)
            wait_all(copies)

        by_parity(body, last)


def finish_kernel(hop, parts, near, far, ze, coef, out_in, out, done, sem):
    del out_in
    rows = ze.shape[1]
    lon, lev = coef.shape[1:3]

    @pl.when(lax.axis_index("tm") == hop + 1)
    def _():
        def body(j_near, j_far):
            copies = []
            for j, block in ((j_far, far), (j_near, near)):
                i = 0 if j == 0 else 1
                weight = coef[2 if j == 0 else 1, j]
                for part in range(parts):
                    lo, hi = rows * part // parts, rows * (part + 1) // parts
                    for r in range(lo, hi, lev):
                        done[i, r : r + lev, :] = ze[i, r : r + lev, :] + weight * block[r : r + lev, :]
                    copy = pltpu.make_async_copy(
                        done.at[i, lo:hi, :], out.at[lo:hi, j, :], sem.at[i * parts + part]
                    )
                    copy.start()
                    copies.append(copy)
            wait_all(copies)

        by_parity(body, lon - 1)


def call(kernel, out_shape, in_specs, out_specs, scratch, semaphores, aliases=None):
    room = sum(4 * math.prod(ref.inner_aval.shape) for ref in scratch)
    return pl.pallas_call(
        kernel,
        out_shape=out_shape,
        in_specs=in_specs,
        out_specs=out_specs,
        scratch_shapes=scratch + [pltpu.SemaphoreType.DMA((count,)) for count in semaphores],
        compiler_params=pltpu.CompilerParams(vmem_limit_bytes=room + 2**22),
        input_output_aliases=aliases or {},
    )


def advance(hop, state, traj, land_mask, coupling):
    rows, lon, lat = state.shape
    lev = traj.shape[1]
    n = lax.axis_size("space")
    f32 = jnp.float32

    def buffer(*dims, dtype=f32):
        return pltpu.VMEM(dims, dtype)

    def in_vmem(array):
        return pltpu.with_memory_space_constraint(array, pltpu.VMEM)

    def in_hbm(array):
        return pltpu.with_memory_space_constraint(array, pltpu.HBM)

    def moved(block, move):
        pairs = [(hop * n + s, (hop + 1) * n + move(s) % n) for s in range(n)]
        pairs += [((hop + 1) * n + s, hop * n + s) for s in range(n)]
        pairs += [(r, r) for r in range(lax.axis_size("tm") * n) if r // n not in (hop, hop + 1)]
        block = lax.ppermute(block, ("tm", "space"), pairs)
        return in_vmem(block)

    def to_near(s):
        return s + 1 if s % 2 == 0 else s - 1

    def to_far(s):
        return s - 1 if s % 2 == 0 else s + 1

    coupling = in_vmem(coupling)
    held = in_hbm(state), in_hbm(traj), in_hbm(land_mask)
    near, far = call(
        functools.partial(edges_kernel, hop),
        [buffer(rows + lev, lat)] * 2,
        [HBM] * 3,
        [VMEM] * 2,
        [buffer(2, lev, lat), buffer(2, lev, lat, dtype=jnp.int32)],
        [6],
    )(*held)
    near_x = moved(near, to_near)
    far_x = moved(far, to_far)
    packed = call(
        functools.partial(pack_kernel, hop),
        buffer(lon, rows + 3 * lev, lat),
        [HBM] * 3 + [VMEM] * 2,
        VMEM,
        [buffer(lon, lev, lat, dtype=jnp.int32)],
        [4 * lon - 2],
    )(*held, in_vmem(near), in_vmem(far))
    sent = moved(packed, lambda s: s)
    packed = in_vmem(packed)
    packed = in_vmem(packed)

    def partial(side):
        return call(
            functools.partial(partial_kernel, hop, side == "far"),
            buffer(rows, lat),
            [VMEM] * 2,
            VMEM,
            [],
            [],
        )(packed, coupling)

    far_p = moved(partial("far"), to_far)
    near_p = moved(partial("near"), to_near)
    z, coef = call(
        functools.partial(main_kernel, hop),
        [buffer(lon, rows, lat), buffer(5, lon, lev, lat)],
        [HBM] + [VMEM] * 2,
        [VMEM] * 2,
        [buffer(lon, rows, lat)],
        [lon],
    )(held[0], sent, coupling)
    z, coef = in_vmem(z), in_vmem(coef)
    out = jax.ShapeDtypeStruct(state.shape, f32)
    state, ze = call(
        functools.partial(sides_kernel, hop),
        [out, buffer(2, rows, lat)],
        [HBM] + [VMEM] * 7,
        [HBM, VMEM],
        [buffer(lon - 2, rows, lat)],
        [lon],
    )(held[0], packed, sent, coupling, near_x, far_x, z, coef)
    parts = 2
    state = call(
        functools.partial(finish_kernel, hop, parts),
        out,
        [VMEM] * 4 + [HBM],
        HBM,
        [buffer(2, rows, lat)],
        [2 * parts],
        {4: 0},
    )(near_p, far_p, in_vmem(ze), coef, in_hbm(state))
    return state


def per_device(forcing, trajectory, land_mask, coupling):
    _, mem, var, lev, lon, lat = forcing.shape
    assert lax.axis_size("space") % 2 == 0 and lon >= 3 and STEPS == 2
    state = forcing.reshape(mem * var * lev, lon, lat)
    for hop in range(lax.axis_size("tm") - 1):
        state = advance(hop, state, trajectory[0], land_mask, coupling)
    return state.reshape(forcing.shape)


def solution(mesh):
    return jax.shard_map(
        per_device,
        mesh=mesh,
        in_specs=(
            P("tm", None, None, None, "space", None),
            P("tm", None, None, "space", None),
            P(None, "space", None),
            P(),
        ),
        out_specs=P("tm", None, None, None, "space", None),
        check_vma=False,
    )
```

time: 23.7 us -> 22.9 us (0.966)
  the two profiles are of different devices: /device:TPU:1 before, /device:TPU:3 now
where the time goes in v3:
time: 22.9 us; the launch traced here: 22.8 us
  waiting for transfers between devices  11.7 us (51%)
  starting transfers between devices  6.22 us (27%)
  Pallas kernels  4.76 us (21%)
    ppermute x5, waiting for transfers between devices, moved(): block = lax.ppermute(block, ('tm', 'space'), pairs)  11.7 us
    ppermute x5, starting transfers between devices, moved(): block = lax.ppermute(block, ('tm', 'space'), pairs)  6.22 us
    pallas_call x1, Pallas kernels, advance(): call(functools.partial(main_kernel, hop), [buffer(lon, rows, lat), buffer...  2.55 us
    pallas_call x1, Pallas kernels, advance(): call(functools.partial(sides_kernel, hop), [out, buffer(2, rows, lat)], [...  1.13 us
    pallas_call x1, Pallas kernels, advance(): call(functools.partial(finish_kernel, hop, parts), out, [VMEM] * 4 + [HBM...  0.89 us
  transfers between devices with their start and end apart: 5, of which 3 were waited for; matrix products, arithmetic and copies ran while one was open for 0% of the time, Pallas kernels for 16%

profile of v3, /device:TPU:3, one launch (start us, length us, event | category | flops | bytes accessed | tf_op | source)
XLA Modules:
  0.0 22.8 jit_solution(13820902851597287337)
XLA Ops:
  0.0 0.1 shard_map.46
  0.1 0.0 copy-start
  0.1 0.1 shard_map.47.packed
  0.2 3.2 %collective-permute-start.2 = (f32[4,152,640]{2,1,0:T(8,128)S(1)}, f32[4,152,640]{2,1,0:T(8,128)S(1)}, u32[]{:S(2)}, u32[]{:S(2)}) collective-permute-start(f32[4,152,640]{2,1,0:T(8,128)S(1)} %shard_map.47.packed), channel_id=1, source_target_pairs={{0,16},{1,17},{2,18},{3,19},{4,20},{5,21},{6,22},{7,23},{8,24},{9,... | collective-permute-start | bytes 4669448 | tf_op jit(solution)/shard_map/ppermute | solution.py:327
  3.5 0.1 collective-permute-start.3
  3.5 0.1 collective-permute-start.4
  3.6 0.0 copy-done
  3.6 2.2 %collective-permute-start = (f32[128,640]{1,0:T(8,128)S(1)}, f32[128,640]{1,0:T(8,128)S(1)}, u32[]{:S(2)}, u32[]{:S(2)}) collective-permute-start(f32[128,640]{1,0:T(8,128)S(1)} %shard_map.48), channel_id=1, source_target_pairs={{0,17},{1,16},{2,19},{3,18},{4,21},{5,20},{6,23},{7,22},{8,25},{9,... | collective-permute-start | bytes 983048 | tf_op jit(solution)/shard_map/ppermute | solution.py:327
  5.8 0.7 %collective-permute-start.1 = (f32[128,640]{1,0:T(8,128)S(1)}, f32[128,640]{1,0:T(8,128)S(1)}, u32[]{:S(2)}, u32[]{:S(2)}) collective-permute-start(f32[128,640]{1,0:T(8,128)S(1)} %shard_map.49), channel_id=1, source_target_pairs={{0,31},{1,18},{2,17},{3,20},{4,19},{5,22},{6,21},{7,24},{8,23},{9,... | collective-permute-start | bytes 983048 | tf_op jit(solution)/shard_map/ppermute | solution.py:327
  6.5 0.0 collective-permute-done.2.sent
  6.5 2.5 %shard_map.50 = (f32[4,128,640]{2,1,0:T(8,128)S(1)}, f32[5,4,8,640]{3,2,1,0:T(8,128)S(1)}) custom-call(f32[128,4,640]{2,1,0:T(4,128)} %bitcast.5, f32[4,152,640]{2,1,0:T(8,128)S(1)} %collective-permute-done.2.sent, f32[4,4]{1,0:T(4,128)S(1)} %copy-done), custom_call_target="tpu_custom_call" | custom-call | tf_op jit(solution)/shard_map/pallas_call | solution.py:372
  9.0 8.4 %collective-permute-done.3.near = f32[136,640]{1,0:T(8,128)S(1)} collective-permute-done((f32[136,640]{1,0:T(8,128)S(1)}, f32[136,640]{1,0:T(8,128)S(1)}, u32[]{:S(2)}, u32[]{:S(2)}) %collective-permute-start.3) | collective-permute-done | bytes 348192 | tf_op jit(solution)/shard_map/ppermute | solution.py:327
  17.4 0.0 collective-permute-done.4.far
  17.4 1.1 %shard_map.51 = (f32[128,4,640]{2,1,0:T(4,128)}, f32[2,128,640]{2,1,0:T(8,128)S(1)}) custom-call(f32[128,4,640]{2,1,0:T(4,128)} %bitcast.6, f32[4,152,640]{2,1,0:T(8,128)S(1)} %shard_map.47.packed, f32[4,152,640]{2,1,0:T(8,128)S(1)} %collective-permute-done.2.sent, f32[4,4]{1,0:T(4,128)S(1)} %copy-done, f32[136,640]{1,0:T(8,128)S(1)} %collective-permute-done.3.near, ...), custom_call_target="tpu_custom_call" | custom-call | tf_op jit(solution)/shard_map/pallas_call | solution.py:382
  18.6 2.4 %collective-permute-done.near = f32[128,640]{1,0:T(8,128)S(1)} collective-permute-done((f32[128,640]{1,0:T(8,128)S(1)}, f32[128,640]{1,0:T(8,128)S(1)}, u32[]{:S(2)}, u32[]{:S(2)}) %collective-permute-start) | collective-permute-done | bytes 327712 | tf_op jit(solution)/shard_map/ppermute | solution.py:327
  20.9 1.0 %collective-permute-done.1.far = f32[128,640]{1,0:T(8,128)S(1)} collective-permute-done((f32[128,640]{1,0:T(8,128)S(1)}, f32[128,640]{1,0:T(8,128)S(1)}, u32[]{:S(2)}, u32[]{:S(2)}) %collective-permute-start.1) | collective-permute-done | bytes 327712 | tf_op jit(solution)/shard_map/ppermute | solution.py:327
  21.9 0.9 %shard_map.52 = f32[128,4,640]{2,1,0:T(4,128)} custom-call(f32[128,640]{1,0:T(8,128)S(1)} %collective-permute-done.near, f32[128,640]{1,0:T(8,128)S(1)} %collective-permute-done.1.far, f32[2,128,640]{2,1,0:T(8,128)S(1)} %get-tuple-element.15.ze, f32[5,4,8,640]{3,2,1,0:T(8,128)S(1)} %get-tuple-element.14.coef, ...), custom_call_target="tpu_custom_call", output_to_operand_aliasing={{}: (4, {})} | custom-call | tf_op jit(solution)/shard_map/pallas_call | solution.py:391
  (2 shorter events, 0.0 us)
Async XLA Ops:
  0.1 3.5 %copy-start = (f32[4,4]{1,0:T(4,128)S(1)}, f32[4,4]{1,0:T(4,128)}, u32[]{:S(2)}) copy-start(f32[4,4]{1,0:T(4,128)} %coupling.7) | copy-start | bytes 196
  0.2 6.3 %collective-permute-start.2 = (f32[4,152,640]{2,1,0:T(8,128)S(1)}, f32[4,152,640]{2,1,0:T(8,128)S(1)}, u32[]{:S(2)}, u32[]{:S(2)}) collective-permute-start(f32[4,152,640]{2,1,0:T(8,128)S(1)} %shard_map.47.packed), channel_id=1, source_target_pairs={{0,16},{1,17},{2,18},{3,19},{4,20},{5,21},{6,22},{7,23},{8,24},{9,... | collective-permute-start | bytes 4669448 | tf_op jit(solution)/shard_map/ppermute | solution.py:327
  3.5 14.0 %collective-permute-start.3 = (f32[136,640]{1,0:T(8,128)S(1)}, f32[136,640]{1,0:T(8,128)S(1)}, u32[]{:S(2)}, u32[]{:S(2)}) collective-permute-start(f32[136,640]{1,0:T(8,128)S(1)} %get-tuple-element.11.near), channel_id=1, source_target_pairs={{0,17},{1,16},{2,19},{3,18},{4,21},{5,20},{6,23},{7,22},{8,25},{9,... | collective-permute-start | bytes 1044488 | tf_op jit(solution)/shard_map/ppermute | solution.py:327
  3.5 13.9 %collective-permute-start.4 = (f32[136,640]{1,0:T(8,128)S(1)}, f32[136,640]{1,0:T(8,128)S(1)}, u32[]{:S(2)}, u32[]{:S(2)}) collective-permute-start(f32[136,640]{1,0:T(8,128)S(1)} %get-tuple-element.12.far), channel_id=1, source_target_pairs={{0,31},{1,18},{2,17},{3,20},{4,19},{5,22},{6,21},{7,24},{8,23},{9,... | collective-permute-start | bytes 1044488 | tf_op jit(solution)/shard_map/ppermute | solution.py:327
  3.6 17.3 %collective-permute-start = (f32[128,640]{1,0:T(8,128)S(1)}, f32[128,640]{1,0:T(8,128)S(1)}, u32[]{:S(2)}, u32[]{:S(2)}) collective-permute-start(f32[128,640]{1,0:T(8,128)S(1)} %shard_map.48), channel_id=1, source_target_pairs={{0,17},{1,16},{2,19},{3,18},{4,21},{5,20},{6,23},{7,22},{8,25},{9,... | collective-permute-start | bytes 983048 | tf_op jit(solution)/shard_map/ppermute | solution.py:327
  5.8 16.1 %collective-permute-start.1 = (f32[128,640]{1,0:T(8,128)S(1)}, f32[128,640]{1,0:T(8,128)S(1)}, u32[]{:S(2)}, u32[]{:S(2)}) collective-permute-start(f32[128,640]{1,0:T(8,128)S(1)} %shard_map.49), channel_id=1, source_target_pairs={{0,31},{1,18},{2,17},{3,20},{4,19},{5,22},{6,21},{7,24},{8,23},{9,... | collective-permute-start | bytes 983048 | tf_op jit(solution)/shard_map/ppermute | solution.py:327

commit v4 on v3

--- a/solution.py
+++ b/solution.py
@@ -71,57 +71,60 @@
         return stencil(u, v, nu)
 
 
-def edges_kernel(hop, x, traj, mask, near, far, wind, open_, sem):
+def entry_weight(j, u, mask):
+    nu, half = 0.15 * mask.astype(jnp.float32), 0.5 * u
+    return nu + half if j == 0 else nu - half
+
+
+def edge_kernel(hop, x, traj, mask, near, wind, open_, sem):
     rows = x.shape[0]
-    last = x.shape[1] - 1
 
     @pl.when(lax.axis_index("tm") == hop)
     def _():
-        others = []
-        for i, j in enumerate((0, last)):
-            others.append((traj.at[0, :, j, :], wind.at[i]))
-            others.append((mask.at[:, j, :], open_.at[i]))
-
         def fill(j_near, j_far):
-            fields = [(x.at[:, j, :], ref.at[0:rows, :]) for j, ref in ((j_near, near), (j_far, far))]
-            copies = run_copies(others + fields, sem)
-            wait_all(copies[: len(others)])
-            for j, ref in ((j_near, near), (j_far, far)):
-                i = 0 if j == 0 else 1
-                nu, half = 0.15 * open_[i].astype(jnp.float32), 0.5 * wind[i]
-                ref[rows:, :] = nu + half if j == 0 else nu - half
-            wait_all(copies[len(others) :])
-
-        by_parity(fill, last)
-
-
-def pack_kernel(hop, x, traj, mask, near, far, packed, open_, sem):
+            pairs = [
+                (x.at[:, j_near, :], near.at[0:rows, :]),
+                (traj.at[0, :, j_near, :], wind),
+                (mask.at[:, j_near, :], open_),
+            ]
+            copies = run_copies(pairs, sem)
+            wait_all(copies[1:])
+            near[rows:, :] = entry_weight(j_near, wind[...], open_[...])
+            wait_all(copies[:1])
+
+        by_parity(fill, x.shape[1] - 1)
+
+
+def pack_kernel(hop, x, traj, mask, near, packed, far, open_, sem):
     rows, lon = x.shape[0], x.shape[1]
     lev = traj.shape[1]
     last = lon - 1
 
     @pl.when(lax.axis_index("tm") == hop)
     def _():
-        pairs = []
-        for j in range(lon):
-            pairs.append((mask.at[:, j, :], open_.at[j]))
-        for j in range(lon):
-            for k in range(2):
-                start = rows + k * lev
-                pairs.append((traj.at[k, :, j, :], packed.at[j, start : start + lev, :]))
-        pairs += [(x.at[:, j, :], packed.at[j, 0:rows, :]) for j in range(1, last)]
-        copies = run_copies(pairs, sem)
-
         def fill(j_near, j_far):
-            for j, ref in ((j_near, near), (j_far, far)):
-                for r in range(0, rows, lev):
-                    packed[j, r : r + lev, :] = ref[r : r + lev, :]
+            masks = [(mask.at[:, j, :], open_.at[j]) for j in range(lon)]
+            wind = []
+            for j in range(lon):
+                for k in range(2):
+                    start = rows + k * lev
+                    wind.append((traj.at[k, :, j, :], packed.at[j, start : start + lev, :]))
+            others = [j_far] + [j for j in range(1, last)]
+            fields = [(x.at[:, j, :], packed.at[j, 0:rows, :]) for j in others]
+            copies = run_copies(masks + wind + fields, sem)
+            for r in range(0, rows, lev):
+                packed[j_near, r : r + lev, :] = near[r : r + lev, :]
+            small = len(masks) + len(wind)
+            wait_all(copies[:small])
+            for j in range(lon):
+                packed[j, rows + 2 * lev :, :] = 0.15 * open_[j].astype(jnp.float32)
+            far[rows:, :] = entry_weight(j_far, packed[j_far, rows : rows + lev, :], open_[j_far])
+            wait_all(copies[small : small + 1])
+            for r in range(0, rows, lev):
+                far[r : r + lev, :] = packed[j_far, r : r + lev, :]
+            wait_all(copies[small + 1 :])
 
         by_parity(fill, last)
-        wait_all(copies[:lon])
-        for j in range(lon):
-            packed[j, rows + 2 * lev :, :] = 0.15 * open_[j].astype(jnp.float32)
-        wait_all(copies[lon:])
 
 
 def partial_kernel(hop, to_far, packed, coupling, out):
@@ -335,24 +338,24 @@
 
     coupling = in_vmem(coupling)
     held = in_hbm(state), in_hbm(traj), in_hbm(land_mask)
-    near, far = call(
-        functools.partial(edges_kernel, hop),
-        [buffer(rows + lev, lat)] * 2,
+    near = call(
+        functools.partial(edge_kernel, hop),
+        buffer(rows + lev, lat),
         [HBM] * 3,
-        [VMEM] * 2,
-        [buffer(2, lev, lat), buffer(2, lev, lat, dtype=jnp.int32)],
-        [6],
+        VMEM,
+        [buffer(lev, lat), buffer(lev, lat, dtype=jnp.int32)],
+        [3],
     )(*held)
     near_x = moved(near, to_near)
+    packed, far = call(
+        functools.partial(pack_kernel, hop),
+        [buffer(lon, rows + 3 * lev, lat), buffer(rows + lev, lat)],
+        [HBM] * 3 + [VMEM],
+        [VMEM] * 2,
+        [buffer(lon, lev, lat, dtype=jnp.int32)],
+        [4 * lon - 1],
+    )(*held, in_vmem(near))
     far_x = moved(far, to_far)
-    packed = call(
-        functools.partial(pack_kernel, hop),
-        buffer(lon, rows + 3 * lev, lat),
-        [HBM] * 3 + [VMEM] * 2,
-        VMEM,
-        [buffer(lon, lev, lat, dtype=jnp.int32)],
-        [4 * lon - 2],
-    )(*held, in_vmem(near), in_vmem(far))
     sent = moved(packed, lambda s: s)
     packed = in_vmem(packed)
     packed = in_vmem(packed)

time: 22.9 us -> 23.8 us (1.039)
  starting transfers between devices: 6.22 us -> 10.1 us
  waiting for transfers between devices: 11.7 us -> 8.71 us
    ppermute x5, starting transfers between devices: 6.22 us -> 10.1 us  [moved(): block = lax.ppermute(block, ('tm', 'space'), pairs)]
    ppermute x5, waiting for transfers between devices: 11.7 us -> 8.71 us  [moved(): block = lax.ppermute(block, ('tm', 'space'), pairs)]
  transfers between devices with their start and end apart: 5 -> 5, of which waited for: 3 -> 2; matrix products, arithmetic and copies ran while one was open for 0% -> 0% of each run, Pallas kernels for 16% -> 16%
where the time goes in v4:
time: 23.8 us; the launch traced here: 23.6 us
  starting transfers between devices  10.1 us (42%)
  waiting for transfers between devices  8.71 us (37%)
  Pallas kernels  4.77 us (20%)
    ppermute x5, starting transfers between devices, moved(): block = lax.ppermute(block, ('tm', 'space'), pairs)  10.1 us
    ppermute x5, waiting for transfers between devices, moved(): block = lax.ppermute(block, ('tm', 'space'), pairs)  8.71 us
    pallas_call x1, Pallas kernels, advance(): call(functools.partial(main_kernel, hop), [buffer(lon, rows, lat), buffer...  2.57 us
    pallas_call x1, Pallas kernels, advance(): call(functools.partial(sides_kernel, hop), [out, buffer(2, rows, lat)], [...  1.13 us
    pallas_call x1, Pallas kernels, advance(): call(functools.partial(finish_kernel, hop, parts), out, [VMEM] * 4 + [HBM...  0.89 us
  transfers between devices with their start and end apart: 5, of which 2 were waited for; matrix products, arithmetic and copies ran while one was open for 0% of the time, Pallas kernels for 16%

profile of v4, /device:TPU:3, one launch (start us, length us, event | category | flops | bytes accessed | tf_op | source)
XLA Modules:
  0.0 23.6 jit_solution(4410363994453355011)
XLA Ops:
  0.0 0.0 copy-start
  0.0 0.2 shard_map.47
  0.2 3.2 %collective-permute-start.2 = (f32[4,152,640]{2,1,0:T(8,128)S(1)}, f32[4,152,640]{2,1,0:T(8,128)S(1)}, u32[]{:S(2)}, u32[]{:S(2)}) collective-permute-start(f32[4,152,640]{2,1,0:T(8,128)S(1)} %get-tuple-element.11.packed), channel_id=1, source_target_pairs={{0,16},{1,17},{2,18},{3,19},{4,20},{5,21},{6,22},{7,23},{8,24},{9,... | collective-permute-start | bytes 4669448 | tf_op jit(solution)/shard_map/ppermute | solution.py:330
  3.4 0.1 collective-permute-start.4
  3.5 1.5 %collective-permute-start.3 = (f32[136,640]{1,0:T(8,128)S(1)}, f32[136,640]{1,0:T(8,128)S(1)}, u32[]{:S(2)}, u32[]{:S(2)}) collective-permute-start(f32[136,640]{1,0:T(8,128)S(1)} %shard_map.46.near), channel_id=1, source_target_pairs={{0,17},{1,16},{2,19},{3,18},{4,21},{5,20},{6,23},{7,22},{8,25},{9,... | collective-permute-start | bytes 1044488 | tf_op jit(solution)/shard_map/ppermute | solution.py:330
  5.0 0.0 copy-done
  5.0 0.6 %collective-permute-start = (f32[128,640]{1,0:T(8,128)S(1)}, f32[128,640]{1,0:T(8,128)S(1)}, u32[]{:S(2)}, u32[]{:S(2)}) collective-permute-start(f32[128,640]{1,0:T(8,128)S(1)} %shard_map.48), channel_id=1, source_target_pairs={{0,17},{1,16},{2,19},{3,18},{4,21},{5,20},{6,23},{7,22},{8,25},{9,... | collective-permute-start | bytes 983048 | tf_op jit(solution)/shard_map/ppermute | solution.py:330
  5.6 4.6 %collective-permute-start.1 = (f32[128,640]{1,0:T(8,128)S(1)}, f32[128,640]{1,0:T(8,128)S(1)}, u32[]{:S(2)}, u32[]{:S(2)}) collective-permute-start(f32[128,640]{1,0:T(8,128)S(1)} %shard_map.49), channel_id=1, source_target_pairs={{0,31},{1,18},{2,17},{3,20},{4,19},{5,22},{6,21},{7,24},{8,23},{9,... | collective-permute-start | bytes 983048 | tf_op jit(solution)/shard_map/ppermute | solution.py:330
  10.3 0.0 collective-permute-done.2.sent
  10.3 2.6 %shard_map.50 = (f32[4,128,640]{2,1,0:T(8,128)S(1)}, f32[5,4,8,640]{3,2,1,0:T(8,128)S(1)}) custom-call(f32[128,4,640]{2,1,0:T(4,128)} %bitcast.5, f32[4,152,640]{2,1,0:T(8,128)S(1)} %collective-permute-done.2.sent, f32[4,4]{1,0:T(4,128)S(1)} %copy-done), custom_call_target="tpu_custom_call" | custom-call | tf_op jit(solution)/shard_map/pallas_call | solution.py:375
  12.9 0.0 collective-permute-done.4.far
  12.9 6.3 %collective-permute-done.3.near = f32[136,640]{1,0:T(8,128)S(1)} collective-permute-done((f32[136,640]{1,0:T(8,128)S(1)}, f32[136,640]{1,0:T(8,128)S(1)}, u32[]{:S(2)}, u32[]{:S(2)}) %collective-permute-start.3) | collective-permute-done | bytes 348192 | tf_op jit(solution)/shard_map/ppermute | solution.py:330
  19.2 1.1 %shard_map.51 = (f32[128,4,640]{2,1,0:T(4,128)}, f32[2,128,640]{2,1,0:T(8,128)S(1)}) custom-call(f32[128,4,640]{2,1,0:T(4,128)} %bitcast.6, f32[4,152,640]{2,1,0:T(8,128)S(1)} %get-tuple-element.11.packed, f32[4,152,640]{2,1,0:T(8,128)S(1)} %collective-permute-done.2.sent, f32[4,4]{1,0:T(4,128)S(1)} %copy-done, f32[136,640]{1,0:T(8,128)S(1)} %collective-permute-done.3.near, ...), custom_call_target="tpu_custom_call" | custom-call | tf_op jit(solution)/shard_map/pallas_call | solution.py:385
  20.3 2.4 %collective-permute-done.near = f32[128,640]{1,0:T(8,128)S(1)} collective-permute-done((f32[128,640]{1,0:T(8,128)S(1)}, f32[128,640]{1,0:T(8,128)S(1)}, u32[]{:S(2)}, u32[]{:S(2)}) %collective-permute-start) | collective-permute-done | bytes 327712 | tf_op jit(solution)/shard_map/ppermute | solution.py:330
  22.7 0.0 collective-permute-done.1.far
  22.7 0.9 %shard_map.52 = f32[128,4,640]{2,1,0:T(4,128)} custom-call(f32[128,640]{1,0:T(8,128)S(1)} %collective-permute-done.near, f32[128,640]{1,0:T(8,128)S(1)} %collective-permute-done.1.far, f32[2,128,640]{2,1,0:T(8,128)S(1)} %get-tuple-element.15.ze, f32[5,4,8,640]{3,2,1,0:T(8,128)S(1)} %get-tuple-element.14.coef, ...), custom_call_target="tpu_custom_call", output_to_operand_aliasing={{}: (4, {})} | custom-call | tf_op jit(solution)/shard_map/pallas_call | solution.py:394
  (3 shorter events, 0.0 us)
Async XLA Ops:
  0.0 5.0 %copy-start = (f32[4,4]{1,0:T(4,128)S(1)}, f32[4,4]{1,0:T(4,128)}, u32[]{:S(2)}) copy-start(f32[4,4]{1,0:T(4,128)} %coupling.7) | copy-start | bytes 196
  0.2 10.1 %collective-permute-start.2 = (f32[4,152,640]{2,1,0:T(8,128)S(1)}, f32[4,152,640]{2,1,0:T(8,128)S(1)}, u32[]{:S(2)}, u32[]{:S(2)}) collective-permute-start(f32[4,152,640]{2,1,0:T(8,128)S(1)} %get-tuple-element.11.packed), channel_id=1, source_target_pairs={{0,16},{1,17},{2,18},{3,19},{4,20},{5,21},{6,22},{7,23},{8,24},{9,... | collective-permute-start | bytes 4669448 | tf_op jit(solution)/shard_map/ppermute | solution.py:330
  3.4 9.5 %collective-permute-start.4 = (f32[136,640]{1,0:T(8,128)S(1)}, f32[136,640]{1,0:T(8,128)S(1)}, u32[]{:S(2)}, u32[]{:S(2)}) collective-permute-start(f32[136,640]{1,0:T(8,128)S(1)} %get-tuple-element.12), channel_id=1, source_target_pairs={{0,31},{1,18},{2,17},{3,20},{4,19},{5,22},{6,21},{7,24},{8,23},{9,... | collective-permute-start | bytes 1044488 | tf_op jit(solution)/shard_map/ppermute | solution.py:330
  3.5 15.7 %collective-permute-start.3 = (f32[136,640]{1,0:T(8,128)S(1)}, f32[136,640]{1,0:T(8,128)S(1)}, u32[]{:S(2)}, u32[]{:S(2)}) collective-permute-start(f32[136,640]{1,0:T(8,128)S(1)} %shard_map.46.near), channel_id=1, source_target_pairs={{0,17},{1,16},{2,19},{3,18},{4,21},{5,20},{6,23},{7,22},{8,25},{9,... | collective-permute-start | bytes 1044488 | tf_op jit(solution)/shard_map/ppermute | solution.py:330
  5.0 17.7 %collective-permute-start = (f32[128,640]{1,0:T(8,128)S(1)}, f32[128,640]{1,0:T(8,128)S(1)}, u32[]{:S(2)}, u32[]{:S(2)}) collective-permute-start(f32[128,640]{1,0:T(8,128)S(1)} %shard_map.48), channel_id=1, source_target_pairs={{0,17},{1,16},{2,19},{3,18},{4,21},{5,20},{6,23},{7,22},{8,25},{9,... | collective-permute-start | bytes 983048 | tf_op jit(solution)/shard_map/ppermute | solution.py:330
  5.6 17.1 %collective-permute-start.1 = (f32[128,640]{1,0:T(8,128)S(1)}, f32[128,640]{1,0:T(8,128)S(1)}, u32[]{:S(2)}, u32[]{:S(2)}) collective-permute-start(f32[128,640]{1,0:T(8,128)S(1)} %shard_map.49), channel_id=1, source_target_pairs={{0,31},{1,18},{2,17},{3,20},{4,19},{5,22},{6,21},{7,24},{8,23},{9,... | collective-permute-start | bytes 983048 | tf_op jit(solution)/shard_map/ppermute | solution.py:330

commit v5 on v4

--- a/solution.py
+++ b/solution.py
@@ -127,9 +127,10 @@
         by_parity(fill, last)
 
 
-def partial_kernel(hop, to_far, packed, coupling, out):
+def partial_kernel(hop, to_far, packed, coupling, *outs):
     last = packed.shape[0] - 1
-    rows, var = out.shape[0], coupling.shape[0]
+    var = coupling.shape[0]
+    rows = sum(out.shape[0] for out in outs)
     lev = (packed.shape[1] - rows) // 3
 
     @pl.when(lax.axis_index("tm") == hop)
@@ -142,18 +143,21 @@
             inner = Packed(packed, 1 if j == 0 else last - 1, rows, lev)
             mid, east, west, north, south = here.weights()
             side = east if j == 0 else west
-
-            def member(m, carry):
-                base = pl.multiple_of(m * var * lev, lev)
-                block = [here.field(base + d * lev) for d in range(var)]
-                for c in range(var):
-                    up, low = shifts(block[c])
-                    total = mid * block[c] + side * inner.field(base + c * lev)
-                    total += north * up + south * low
-                    out[pl.ds(base + c * lev, lev), :] = total + mix(pair, block, c)
-                return carry
-
-            lax.fori_loop(0, rows // (var * lev), member, 0)
+            lo = 0
+            for out in outs:
+
+                def member(m, carry, lo=lo, out=out):
+                    base = pl.multiple_of(m * var * lev, lev)
+                    block = [here.field(lo + base + d * lev) for d in range(var)]
+                    for c in range(var):
+                        up, low = shifts(block[c])
+                        total = mid * block[c] + side * inner.field(lo + base + c * lev)
+                        total += north * up + south * low
+                        out[pl.ds(base + c * lev, lev), :] = total + mix(pair, block, c)
+                    return carry
+
+                lax.fori_loop(0, out.shape[0] // (var * lev), member, 0, unroll=True)
+                lo += out.shape[0]
 
         by_parity(send, last)
 
@@ -269,9 +273,9 @@
         by_parity(body, last)
 
 
-def finish_kernel(hop, parts, near, far, ze, coef, out_in, out, done, sem):
+def finish_kernel(hop, lo, near, far, ze, coef, out_in, out, done, sem):
     del out_in
-    rows = ze.shape[1]
+    rows = near.shape[0]
     lon, lev = coef.shape[1:3]
 
     @pl.when(lax.axis_index("tm") == hop + 1)
@@ -281,15 +285,10 @@
             for j, block in ((j_far, far), (j_near, near)):
                 i = 0 if j == 0 else 1
                 weight = coef[2 if j == 0 else 1, j]
-                for part in range(parts):
-                    lo, hi = rows * part // parts, rows * (part + 1) // parts
-                    for r in range(lo, hi, lev):
-                        done[i, r : r + lev, :] = ze[i, r : r + lev, :] + weight * block[r : r + lev, :]
-                    copy = pltpu.make_async_copy(
-                        done.at[i, lo:hi, :], out.at[lo:hi, j, :], sem.at[i * parts + part]
-                    )
-                    copy.start()
-                    copies.append(copy)
+                for r in range(0, rows, lev):
+                    done[i, r : r + lev, :] = ze[i, lo + r : lo + r + lev, :] + weight * block[r : r + lev, :]
+                copies.append(pltpu.make_async_copy(done.at[i], out.at[lo : lo + rows, j, :], sem.at[i]))
+                copies[-1].start()
             wait_all(copies)
 
         by_parity(body, lon - 1)
@@ -310,7 +309,7 @@
 
 def advance(hop, state, traj, land_mask, coupling):
     rows, lon, lat = state.shape
-    lev = traj.shape[1]
+    var, lev = coupling.shape[0], traj.shape[1]
     n = lax.axis_size("space")
     f32 = jnp.float32
 
@@ -360,18 +359,23 @@
     packed = in_vmem(packed)
     packed = in_vmem(packed)
 
-    def partial(side):
-        return call(
+    members = rows // (var * lev)
+    first = members - members // 4
+    sizes = [size * var * lev for size in (first, members - first) if size]
+
+    def partial(side, move):
+        outs = call(
             functools.partial(partial_kernel, hop, side == "far"),
-            buffer(rows, lat),
+            [buffer(size, lat) for size in sizes],
             [VMEM] * 2,
-            VMEM,
+            [VMEM] * len(sizes),
             [],
             [],
         )(packed, coupling)
-
-    far_p = moved(partial("far"), to_far)
-    near_p = moved(partial("near"), to_near)
+        return [moved(block, move) for block in outs]
+
+    near_p = partial("near", to_near)
+    far_p = partial("far", to_far)
     z, coef = call(
         functools.partial(main_kernel, hop),
         [buffer(lon, rows, lat), buffer(5, lon, lev, lat)],
@@ -390,16 +394,17 @@
         [buffer(lon - 2, rows, lat)],
         [lon],
     )(held[0], packed, sent, coupling, near_x, far_x, z, coef)
-    parts = 2
-    state = call(
-        functools.partial(finish_kernel, hop, parts),
-        out,
-        [VMEM] * 4 + [HBM],
-        HBM,
-        [buffer(2, rows, lat)],
-        [2 * parts],
-        {4: 0},
-    )(near_p, far_p, in_vmem(ze), coef, in_hbm(state))
+    ze = in_vmem(ze)
+    for i, size in enumerate(sizes):
+        state = call(
+            functools.partial(finish_kernel, hop, sum(sizes[:i])),
+            out,
+            [VMEM] * 4 + [HBM],
+            HBM,
+            [buffer(2, size, lat)],
+            [2],
+            {4: 0},
+        )(near_p[i], far_p[i], ze, coef, in_hbm(state))
     return state
 
 

time: 23.8 us -> 23.6 us (level)
  waiting for transfers between devices: 8.71 us -> 4.82 us
  starting transfers between devices: 10.1 us -> 13.1 us
  Pallas kernels: 4.77 us -> 5.41 us
    ppermute x5 -> x7, waiting for transfers between devices: 8.71 us -> 4.82 us  [moved(): block = lax.ppermute(block, ('tm', 'space'), pairs)]
    ppermute x5 -> x7, starting transfers between devices: 10.1 us -> 13.1 us  [moved(): block = lax.ppermute(block, ('tm', 'space'), pairs)]
    pallas_call x3 -> x4, Pallas kernels: 0.89 us -> 1.53 us  [the longest x2 1.53 us: advance(): call(functools.partial(finish_kernel, hop, sum(sizes[:i])), out, [VMEM] *...]
  transfers between devices with their start and end apart: 5 -> 7, of which waited for: 2 -> 3; matrix products, arithmetic and copies ran while one was open for 0% -> 0% of each run, Pallas kernels for 16% -> 19%
where the time goes in v5:
time: 23.6 us; the launch traced here: 23.4 us
  starting transfers between devices  13.1 us (56%)
  Pallas kernels  5.41 us (23%)
  waiting for transfers between devices  4.82 us (20%)
    ppermute x7, starting transfers between devices, moved(): block = lax.ppermute(block, ('tm', 'space'), pairs)  13.1 us
    ppermute x7, waiting for transfers between devices, moved(): block = lax.ppermute(block, ('tm', 'space'), pairs)  4.82 us
    pallas_call x1, Pallas kernels, advance(): call(functools.partial(main_kernel, hop), [buffer(lon, rows, lat), buffer...  2.57 us
    pallas_call x2, Pallas kernels, advance(): call(functools.partial(finish_kernel, hop, sum(sizes[:i])), out, [VMEM] *...  1.53 us
    pallas_call x1, Pallas kernels, advance(): call(functools.partial(sides_kernel, hop), [out, buffer(2, rows, lat)], [...  1.13 us
  transfers between devices with their start and end apart: 7, of which 3 were waited for; matrix products, arithmetic and copies ran while one was open for 0% of the time, Pallas kernels for 19%

profile of v5, /device:TPU:3, one launch (start us, length us, event | category | flops | bytes accessed | tf_op | source)
XLA Modules:
  0.0 23.4 jit_solution(14072313957802265987)
XLA Ops:
  0.0 0.0 copy-start
  0.0 0.2 shard_map.47
  0.2 3.2 %collective-permute-start.2 = (f32[4,152,640]{2,1,0:T(8,128)S(1)}, f32[4,152,640]{2,1,0:T(8,128)S(1)}, u32[]{:S(2)}, u32[]{:S(2)}) collective-permute-start(f32[4,152,640]{2,1,0:T(8,128)S(1)} %get-tuple-element.15.packed), channel_id=1, source_target_pairs={{0,16},{1,17},{2,18},{3,19},{4,20},{5,21},{6,22},{7,23},{8,24},{9,... | collective-permute-start | bytes 4669448 | tf_op jit(solution)/shard_map/ppermute | solution.py:329
  3.4 0.1 collective-permute-start.4
  3.5 1.5 %collective-permute-start.3 = (f32[136,640]{1,0:T(8,128)S(1)}, f32[136,640]{1,0:T(8,128)S(1)}, u32[]{:S(2)}, u32[]{:S(2)}) collective-permute-start(f32[136,640]{1,0:T(8,128)S(1)} %shard_map.46.near), channel_id=1, source_target_pairs={{0,17},{1,16},{2,19},{3,18},{4,21},{5,20},{6,23},{7,22},{8,25},{9,... | collective-permute-start | bytes 1044488 | tf_op jit(solution)/shard_map/ppermute | solution.py:329
  5.0 0.0 copy-done
  5.0 0.4 %collective-permute-start.5 = (f32[96,640]{1,0:T(8,128)S(1)}, f32[96,640]{1,0:T(8,128)S(1)}, u32[]{:S(2)}, u32[]{:S(2)}) collective-permute-start(f32[96,640]{1,0:T(8,128)S(1)} %get-tuple-element.22), channel_id=1, source_target_pairs={{0,17},{1,16},{2,19},{3,18},{4,21},{5,20},{6,23},{7,22},{8,25},{9,... | collective-permute-start | bytes 737288 | tf_op jit(solution)/shard_map/ppermute | solution.py:329
  5.4 4.6 %collective-permute-start.6 = (f32[96,640]{1,0:T(8,128)S(1)}, f32[96,640]{1,0:T(8,128)S(1)}, u32[]{:S(2)}, u32[]{:S(2)}) collective-permute-start(f32[96,640]{1,0:T(8,128)S(1)} %get-tuple-element.23), channel_id=1, source_target_pairs={{0,31},{1,18},{2,17},{3,20},{4,19},{5,22},{6,21},{7,24},{8,23},{9,... | collective-permute-start | bytes 737288 | tf_op jit(solution)/shard_map/ppermute | solution.py:329
  10.1 0.9 %collective-permute-done.4.far = f32[136,640]{1,0:T(8,128)S(1)} collective-permute-done((f32[136,640]{1,0:T(8,128)S(1)}, f32[136,640]{1,0:T(8,128)S(1)}, u32[]{:S(2)}, u32[]{:S(2)}) %collective-permute-start.4) | collective-permute-done | bytes 348192 | tf_op jit(solution)/shard_map/ppermute | solution.py:329
  11.0 0.0 collective-permute-start
  11.0 0.0 collective-permute-done.2.sent
  11.0 3.3 %collective-permute-start.1 = (f32[32,640]{1,0:T(8,128)S(1)}, f32[32,640]{1,0:T(8,128)S(1)}, u32[]{:S(2)}, u32[]{:S(2)}) collective-permute-start(f32[32,640]{1,0:T(8,128)S(1)} %get-tuple-element.17), channel_id=1, source_target_pairs={{0,31},{1,18},{2,17},{3,20},{4,19},{5,22},{6,21},{7,24},{8,23},{9,... | collective-permute-start | bytes 245768 | tf_op jit(solution)/shard_map/ppermute | solution.py:329
  14.3 2.6 %shard_map.50 = (f32[4,128,640]{2,1,0:T(8,128)S(1)}, f32[5,4,8,640]{3,2,1,0:T(8,128)S(1)}) custom-call(f32[128,4,640]{2,1,0:T(4,128)} %bitcast.5, f32[4,152,640]{2,1,0:T(8,128)S(1)} %collective-permute-done.2.sent, f32[4,4]{1,0:T(4,128)S(1)} %copy-done), custom_call_target="tpu_custom_call" | custom-call | tf_op jit(solution)/shard_map/pallas_call | solution.py:379
  16.9 2.3 %collective-permute-done.3.near = f32[136,640]{1,0:T(8,128)S(1)} collective-permute-done((f32[136,640]{1,0:T(8,128)S(1)}, f32[136,640]{1,0:T(8,128)S(1)}, u32[]{:S(2)}, u32[]{:S(2)}) %collective-permute-start.3) | collective-permute-done | bytes 348192 | tf_op jit(solution)/shard_map/ppermute | solution.py:329
  19.2 1.1 %shard_map.51 = (f32[128,4,640]{2,1,0:T(4,128)}, f32[2,128,640]{2,1,0:T(8,128)S(1)}) custom-call(f32[128,4,640]{2,1,0:T(4,128)} %bitcast.6, f32[4,152,640]{2,1,0:T(8,128)S(1)} %get-tuple-element.15.packed, f32[4,152,640]{2,1,0:T(8,128)S(1)} %collective-permute-done.2.sent, f32[4,4]{1,0:T(4,128)S(1)} %copy-done, f32[136,640]{1,0:T(8,128)S(1)} %collective-permute-done.3.near, ...), custom_call_target="tpu_custom_call" | custom-call | tf_op jit(solution)/shard_map/pallas_call | solution.py:389
  20.3 1.5 %collective-permute-done.5.near = f32[96,640]{1,0:T(8,128)S(1)} collective-permute-done((f32[96,640]{1,0:T(8,128)S(1)}, f32[96,640]{1,0:T(8,128)S(1)}, u32[]{:S(2)}, u32[]{:S(2)}) %collective-permute-start.5) | collective-permute-done | bytes 245792 | tf_op jit(solution)/shard_map/ppermute | solution.py:329
  21.8 0.0 collective-permute-done.6.far
  21.8 0.8 %shard_map.52.out_in = f32[128,4,640]{2,1,0:T(4,128)} custom-call(f32[96,640]{1,0:T(8,128)S(1)} %collective-permute-done.5.near, f32[96,640]{1,0:T(8,128)S(1)} %collective-permute-done.6.far, f32[2,128,640]{2,1,0:T(8,128)S(1)} %get-tuple-element.21.ze, f32[5,4,8,640]{3,2,1,0:T(8,128)S(1)} %get-tuple-element.20.coef, ...), custom_call_target="tpu_custom_call", output_to_operand_aliasing={{}: (4, {})} | custom-call | tf_op jit(solution)/shard_map/pallas_call | solution.py:399
  22.7 0.0 collective-permute-done.near
  22.7 0.0 collective-permute-done.1.far
  22.7 0.7 %shard_map.53 = f32[128,4,640]{2,1,0:T(4,128)} custom-call(f32[32,640]{1,0:T(8,128)S(1)} %collective-permute-done.near, f32[32,640]{1,0:T(8,128)S(1)} %collective-permute-done.1.far, f32[2,128,640]{2,1,0:T(8,128)S(1)} %get-tuple-element.21.ze, f32[5,4,8,640]{3,2,1,0:T(8,128)S(1)} %get-tuple-element.20.coef, ...), custom_call_target="tpu_custom_call", output_to_operand_aliasing={{}: (4, {})} | custom-call | tf_op jit(solution)/shard_map/pallas_call | solution.py:399
  (3 shorter events, 0.0 us)
Async XLA Ops:
  0.0 5.0 %copy-start = (f32[4,4]{1,0:T(4,128)S(1)}, f32[4,4]{1,0:T(4,128)}, u32[]{:S(2)}) copy-start(f32[4,4]{1,0:T(4,128)} %coupling.7) | copy-start | bytes 196
  0.2 10.8 %collective-permute-start.2 = (f32[4,152,640]{2,1,0:T(8,128)S(1)}, f32[4,152,640]{2,1,0:T(8,128)S(1)}, u32[]{:S(2)}, u32[]{:S(2)}) collective-permute-start(f32[4,152,640]{2,1,0:T(8,128)S(1)} %get-tuple-element.15.packed), channel_id=1, source_target_pairs={{0,16},{1,17},{2,18},{3,19},{4,20},{5,21},{6,22},{7,23},{8,24},{9,... | collective-permute-start | bytes 4669448 | tf_op jit(solution)/shard_map/ppermute | solution.py:329
  3.4 7.6 %collective-permute-start.4 = (f32[136,640]{1,0:T(8,128)S(1)}, f32[136,640]{1,0:T(8,128)S(1)}, u32[]{:S(2)}, u32[]{:S(2)}) collective-permute-start(f32[136,640]{1,0:T(8,128)S(1)} %get-tuple-element.18), channel_id=1, source_target_pairs={{0,31},{1,18},{2,17},{3,20},{4,19},{5,22},{6,21},{7,24},{8,23},{9,... | collective-permute-start | bytes 1044488 | tf_op jit(solution)/shard_map/ppermute | solution.py:329
  3.5 15.7 %collective-permute-start.3 = (f32[136,640]{1,0:T(8,128)S(1)}, f32[136,640]{1,0:T(8,128)S(1)}, u32[]{:S(2)}, u32[]{:S(2)}) collective-permute-start(f32[136,640]{1,0:T(8,128)S(1)} %shard_map.46.near), channel_id=1, source_target_pairs={{0,17},{1,16},{2,19},{3,18},{4,21},{5,20},{6,23},{7,22},{8,25},{9,... | collective-permute-start | bytes 1044488 | tf_op jit(solution)/shard_map/ppermute | solution.py:329
  5.0 16.8 %collective-permute-start.5 = (f32[96,640]{1,0:T(8,128)S(1)}, f32[96,640]{1,0:T(8,128)S(1)}, u32[]{:S(2)}, u32[]{:S(2)}) collective-permute-start(f32[96,640]{1,0:T(8,128)S(1)} %get-tuple-element.22), channel_id=1, source_target_pairs={{0,17},{1,16},{2,19},{3,18},{4,21},{5,20},{6,23},{7,22},{8,25},{9,... | collective-permute-start | bytes 737288 | tf_op jit(solution)/shard_map/ppermute | solution.py:329
  5.4 16.4 %collective-permute-start.6 = (f32[96,640]{1,0:T(8,128)S(1)}, f32[96,640]{1,0:T(8,128)S(1)}, u32[]{:S(2)}, u32[]{:S(2)}) collective-permute-start(f32[96,640]{1,0:T(8,128)S(1)} %get-tuple-element.23), channel_id=1, source_target_pairs={{0,31},{1,18},{2,17},{3,20},{4,19},{5,22},{6,21},{7,24},{8,23},{9,... | collective-permute-start | bytes 737288 | tf_op jit(solution)/shard_map/ppermute | solution.py:329
  11.0 11.7 %collective-permute-start = (f32[32,640]{1,0:T(8,128)S(1)}, f32[32,640]{1,0:T(8,128)S(1)}, u32[]{:S(2)}, u32[]{:S(2)}) collective-permute-start(f32[32,640]{1,0:T(8,128)S(1)} %get-tuple-element.16), channel_id=1, source_target_pairs={{0,17},{1,16},{2,19},{3,18},{4,21},{5,20},{6,23},{7,22},{8,25},{9,... | collective-permute-start | bytes 245768 | tf_op jit(solution)/shard_map/ppermute | solution.py:329
  11.0 11.7 %collective-permute-start.1 = (f32[32,640]{1,0:T(8,128)S(1)}, f32[32,640]{1,0:T(8,128)S(1)}, u32[]{:S(2)}, u32[]{:S(2)}) collective-permute-start(f32[32,640]{1,0:T(8,128)S(1)} %get-tuple-element.17), channel_id=1, source_target_pairs={{0,31},{1,18},{2,17},{3,20},{4,19},{5,22},{6,21},{7,24},{8,23},{9,... | collective-permute-start | bytes 245768 | tf_op jit(solution)/shard_map/ppermute | solution.py:329
